TPU v7x, 1024 devices: a whole 4x8x16 slice. The times are simulated.
1024 devices in a mesh: row: 32 (over x_hi, z), col: 32 (over x_lo, y, core).
Axes of the slice: x: 4 (x_hi: 2, x_lo: 2; x = x_hi * 2 + x_lo), y: 8, z: 16, core: 2. Of those that a mesh axis runs over, the one named last changes fastest.
Arguments:
- queries: bfloat16 [256, 512, 768], P('row', 'col'), may hold values from -6 to 6
- keys: bfloat16 [256, 512, 768], P('row', 'col'), may hold values from -6 to 6
- values: bfloat16 [256, 512, 768], P('row', 'col'), may hold values from -6 to 6
- d_out: bfloat16 [256, 512, 768], P('row', 'col'), may hold values from -6 to 6
- extents: int32 [2, 16, 32], replicated, may hold values from 4 to 16, as said below
- rel_bias: float32 [12, 13, 13], replicated, may hold values from -4 to 4
Outputs:
- attended: bfloat16 [256, 512, 768], P('row', 'col')
- d_queries: bfloat16 [256, 512, 768], P('row', 'col')
- d_keys: bfloat16 [256, 512, 768], P('row', 'col')
- d_values: bfloat16 [256, 512, 768], P('row', 'col')
- d_rel_bias: float32 [12, 13, 13], replicated
Inputs may be any that keep to these rules, and one draw needn't show every extreme that they name: `extents`: every slot holds one image at its top-left corner.
All inputs are finite; a program needn't handle non-finite values.
Results may differ from a plain program's by a relative error of at most 0.011.
Values may be sent and summed in bfloat16 or wider, within the bound.
No kernel may reach another device: no remote copies, remote signals or barrier semaphores. Data moves between devices by JAX's collectives and lax.ppermute only.
A program may use at most 64 MiB of HBM per device.

v0:
```python
import jax
import jax.numpy as jnp
from jax import lax
from jax.sharding import PartitionSpec as P

GROUP = 4


HIGH = lax.Precision.HIGHEST


def from_behind(value, axis, steps):
    count = lax.axis_size(axis)
    initial, last = (max(0, -steps), min(count, count - steps))
    return lax.ppermute(value, axis, [(source, source + steps) for source in range(initial, last)])


def with_halo(value, sides, width):
    for axis, dim in sides:
        size, length = (lax.axis_size(axis), value.shape[dim])
        up = [(i, (i + 1) % size) for i in range(size - 1)]
        down = [(j, i) for i, j in up]
        last = lax.slice_in_dim(value, length - width, length, axis=dim)
        initial = lax.slice_in_dim(value, 0, width, axis=dim)
        before = lax.ppermute(last, axis, up)
        after = lax.ppermute(initial, axis, down)
        value = jnp.concatenate([before, value, after], axis=dim)
    return value


def offset_tables(group_rows, tile_cols, radius):
    span_size = 2 * radius + 1
    query_rows = jnp.arange(group_rows, dtype=jnp.int32)
    key_rows = jnp.arange(group_rows + 2 * radius, dtype=jnp.int32)
    row_offsets = (
        (key_rows[None, :] - query_rows[:, None])[:, :, None]
        == jnp.arange(span_size, dtype=jnp.int32)[None, None, :]
    ).astype(jnp.float32)
    query_cols = jnp.arange(tile_cols, dtype=jnp.int32)
    key_cols = jnp.arange(tile_cols + 2 * radius, dtype=jnp.int32)
    col_offsets = (
        (key_cols[None, :] - query_cols[:, None])[:, :, None]
        == jnp.arange(span_size, dtype=jnp.int32)[None, None, :]
    ).astype(jnp.float32)
    return (row_offsets, col_offsets)


def offset_sum(dscore, row_offsets, col_offsets):
    head_count = dscore.shape[0]
    group_rows, band_rows = (row_offsets.shape[0], row_offsets.shape[1])
    tile_cols, band_cols = (col_offsets.shape[0], col_offsets.shape[1])
    shaped = dscore.reshape(head_count, group_rows, tile_cols, band_rows, band_cols)
    by_col = jnp.einsum("hicjm,cmb->hijb", shaped, col_offsets, precision=HIGH)
    return jnp.einsum("hijb,ija->hab", by_col, row_offsets, precision=HIGH)


def window_valid(extents, tile_rows, tile_cols, radius):
    panel_side = 2 * tile_rows
    canvas_rows = tile_rows * lax.axis_size("row")
    canvas_cols = tile_cols * lax.axis_size("col")
    rows = (
        lax.axis_index("row") * tile_rows
        - radius
        + jnp.arange(tile_rows + 2 * radius, dtype=jnp.int32)
    )
    cols = (
        lax.axis_index("col") * tile_cols
        - radius
        + jnp.arange(tile_cols + 2 * radius, dtype=jnp.int32)
    )
    row_pick = (
        (rows // panel_side)[:, None] == jnp.arange(extents.shape[1], dtype=jnp.int32)[None, :]
    ).astype(jnp.float32)
    col_pick = (
        (cols // panel_side)[:, None] == jnp.arange(extents.shape[2], dtype=jnp.int32)[None, :]
    ).astype(jnp.float32)
    heights = jnp.dot(
        jnp.dot(row_pick, extents[0].astype(jnp.float32), precision=HIGH),
        col_pick.T,
        precision=HIGH,
    )
    widths = jnp.dot(
        jnp.dot(row_pick, extents[1].astype(jnp.float32), precision=HIGH),
        col_pick.T,
        precision=HIGH,
    )
    inside = ((rows >= 0) & (rows < canvas_rows))[:, None] & ((cols >= 0) & (cols < canvas_cols))[
        None, :
    ]
    within = ((rows % panel_side).astype(jnp.float32)[:, None] < heights) & (
        (cols % panel_side).astype(jnp.float32)[None, :] < widths
    )
    return inside & within


def fold_cols(grads, radius):
    inner = grads.shape[2] - 2 * radius
    interior = grads[:, :, radius : radius + inner]
    for direction in (1, -1):
        border = grads[:, :, radius + inner :] if direction == 1 else grads[:, :, :radius]
        arrived = from_behind(border.astype(jnp.bfloat16), "col", direction).astype(border.dtype)
        if direction == 1:
            interior = interior.at[:, :, :radius].add(arrived)
        else:
            interior = interior.at[:, :, inner - radius :].add(arrived)
    return interior


def fold_rows(grads, radius):
    inner = grads.shape[1] - 2 * radius
    interior = grads[:, radius : radius + inner]
    for direction in (1, -1):
        border = grads[:, radius + inner :] if direction == 1 else grads[:, :radius]
        arrived = from_behind(border.astype(jnp.bfloat16), "row", direction).astype(border.dtype)
        if direction == 1:
            interior = interior.at[:, :radius].add(arrived)
        else:
            interior = interior.at[:, inner - radius :].add(arrived)
    return interior


def shards(queries, keys, values, d_out, extents, rel_bias):
    tile_rows, tile_cols, channels = queries.shape
    head_count = rel_bias.shape[0]
    span_size = rel_bias.shape[1]
    radius = (span_size - 1) // 2
    head_size = channels // head_count
    scale = head_size ** (-0.5)
    band_rows = GROUP + 2 * radius
    band_cols = tile_cols + 2 * radius
    padded = with_halo(jnp.stack([keys, values]), (("row", 1), ("col", 2)), radius)
    valid = window_valid(extents, tile_rows, tile_cols, radius)
    row_offsets, col_offsets = offset_tables(GROUP, tile_cols, radius)
    bias = jnp.einsum(
        "hab,ija,cmb->hicjm", rel_bias, row_offsets, col_offsets, precision=HIGH
    ).reshape(head_count, GROUP * tile_cols, band_rows * band_cols)
    window = (
        jnp.sum(row_offsets, -1)[:, None, :, None] * jnp.sum(col_offsets, -1)[None, :, None, :]
        > 0.5
    ).reshape(GROUP * tile_cols, band_rows * band_cols)
    block_count = tile_rows // GROUP
    bias_grad = jnp.zeros((head_count, span_size, span_size), jnp.float32)
    out_pieces = []
    dq_pieces = []
    grad_pieces = []
    high_pieces = []
    total_pieces = []
    delta_pieces = []
    for block in range(block_count):
        first = block * GROUP
        query_heads = queries[first : first + GROUP].reshape(
            GROUP * tile_cols, head_count, head_size
        )
        grad_rows = d_out[first : first + GROUP].reshape(GROUP * tile_cols, head_count, head_size)
        band = padded[:, first : first + band_rows].reshape(
            2, band_rows * band_cols, head_count, head_size
        )
        valid_query = valid[
            first + radius : first + radius + GROUP, radius : radius + tile_cols
        ].reshape(-1)
        valid_key = valid[first : first + band_rows].reshape(-1)

        def group_pass(
            query_heads=query_heads,
            grad_rows=grad_rows,
            band=band,
            valid_query=valid_query,
            valid_key=valid_key,
        ):
            key_heads = band[0]
            value_heads = band[1]
            allowed = window & valid_query[:, None] & valid_key[None, :]
            score = (
                jnp.einsum(
                    "qhd,khd->hqk", query_heads, key_heads, preferred_element_type=jnp.float32
                )
                * scale
                + bias
            )
            score = jnp.where(allowed[None], score, -1e30)
            highest = jnp.max(score, axis=-1, keepdims=True)
            weights = jnp.exp(score - highest)
            total = jnp.sum(weights, axis=-1, keepdims=True)
            prob = weights / total
            prob_b = prob.astype(jnp.bfloat16)
            output = jnp.einsum(
                "hqk,khd->qhd", prob_b, value_heads, preferred_element_type=jnp.float32
            )
            out_block = (
                jnp.where(valid_query[:, None, None], output, 0.0)
                .astype(jnp.bfloat16)
                .reshape(GROUP, tile_cols, channels)
            )
            grad_heads = jnp.where(
                valid_query[:, None, None], grad_rows, jnp.zeros((), jnp.bfloat16)
            )
            delta = jnp.sum(grad_heads.astype(jnp.float32) * output, axis=-1)
            dprob = jnp.einsum(
                "qhd,khd->hqk", grad_heads, value_heads, preferred_element_type=jnp.float32
            )
            dscore = prob * (dprob - jnp.transpose(delta)[:, :, None])
            dscore_b = dscore.astype(jnp.bfloat16)
            dq_block = (
                (
                    jnp.einsum(
                        "hqk,khd->qhd", dscore_b, key_heads, preferred_element_type=jnp.float32
                    )
                    * scale
                )
                .astype(jnp.bfloat16)
                .reshape(GROUP, tile_cols, channels)
            )
            dk_block = (
                jnp.einsum(
                    "hqk,qhd->khd", dscore_b, query_heads, preferred_element_type=jnp.float32
                )
                * scale
            )
            dv_block = jnp.einsum(
                "hqk,qhd->khd", prob_b, grad_heads, preferred_element_type=jnp.float32
            )
            band_grads = jnp.stack([dk_block, dv_block]).reshape(2, band_rows, band_cols, channels)
            bias_part = offset_sum(dscore, row_offsets, col_offsets)
            stats = (
                highest.reshape(head_count, GROUP, tile_cols),
                total.reshape(head_count, GROUP, tile_cols),
                jnp.transpose(delta).reshape(head_count, GROUP, tile_cols),
            )
            return (out_block, dq_block, band_grads, bias_part, stats)

        out_block, dq_block, band_grads, bias_part, stats = group_pass()
        out_pieces.append(out_block)
        dq_pieces.append(dq_block)
        high_pieces.append(stats[0])
        total_pieces.append(stats[1])
        delta_pieces.append(stats[2])
        grad_pieces.append(
            jnp.pad(band_grads, ((0, 0), (first, tile_rows - first - GROUP), (0, 0), (0, 0)))
        )
        bias_grad = bias_grad + bias_part
    grads = grad_pieces[0]
    for piece in grad_pieces[1:]:
        grads = grads + piece
    folded = fold_rows(fold_cols(grads, radius), radius)
    d_keys = folded[0].astype(jnp.bfloat16)
    d_values = folded[1].astype(jnp.bfloat16)
    d_rel_bias = lax.psum(bias_grad, ("row", "col"))
    attended = jnp.concatenate(out_pieces, 0)
    d_queries = jnp.concatenate(dq_pieces, 0)
    return (attended, d_queries, d_keys, d_values, d_rel_bias)


def solution(mesh):
    placed = (
        P("row", "col", None),
        P("row", "col", None),
        P("row", "col", None),
        P("row", "col", None),
        P(),
        P(),
    )
    return jax.shard_map(
        shards,
        mesh=mesh,
        in_specs=placed,
        out_specs=(
            P("row", "col", None),
            P("row", "col", None),
            P("row", "col", None),
            P("row", "col", None),
            P(),
        ),
        check_vma=False,
    )
```

profile of v0, /device:TPU:1, one launch (start us, length us, event | category | flops | bytes accessed | tf_op | source)
XLA Modules:
  0.0 330.1 jit_solution(16052300635963294145)
XLA Ops:
  0.6 2.1 fusion.25
  2.7 1.3 collective-permute-start.1
  4.0 5.5 %collective-permute-start = (bf16[2,6,16,768]{3,2,1,0:T(8,128)(2,1)}, bf16[2,6,16,768]{3,2,1,0:T(8,128)(2,1)S(1)}, u32[]{:S(2)}, u32[]{:S(2)}) collective-permute-start(bf16[2,6,16,768]{3,2,1,0:T(8,128)(2,1)} %get-tuple-element.67), channel_id=1, source_target_pairs={{0,32},{32,64},{64,96},{96,128},{128,160},{160,192},{192,224},{224... | collective-permute-start | bytes 884744 | tf_op jit(solution)/shard_map/ppermute | solution.py:25
  9.5 0.9 fusion.46
  10.4 0.9 fusion.47
  11.8 4.5 %convolution_bitcast_fusion = f32[12,4,16,16,28]{4,3,2,0,1:T(8,128)} fusion(f32[4,16,12,13,1]{3,1,4,2,0:T(8,128)S(1)} %convolution_bitcast_fusion.5, s32[16,28]{1,0:T(8,128)S(1)} %iota_subtract_fusion), kind=kOutput, calls=%fused_computation.7 | convolution fusion | flops 53679808 | bytes 1417984 | tf_op jit(solution)/shard_map/hab,ija,cmb->hicjm/dot_general | solution.py:134
  17.1 6.1 %copy.32 = f32[12,4,16,16,28]{4,3,2,1,0:T(8,128)} copy(f32[12,4,16,16,28]{4,3,2,0,1:T(8,128)} %convolution_bitcast_fusion) | data formatting | bytes 2752512 | tf_op jit(solution)/shard_map/hab,ija,cmb->hicjm/transpose | solution.py:134
  23.2 5.1 %reshape.407 = f32[12,64,448]{2,1,0:T(8,128)S(1)} reshape(f32[12,4,16,16,28]{4,3,2,1,0:T(8,128)} %copy.32) | data formatting | bytes 2752512 | tf_op jit(solution)/shard_map/reshape | solution.py:136
  28.5 0.9 copy.52
  30.5 1.1 fusion.73
  31.6 15.1 %collective-permute-start.3 = (bf16[2,20,6,768]{3,2,1,0:T(8,128)(2,1)}, bf16[2,20,6,768]{3,2,1,0:T(8,128)(2,1)}, u32[]{:S(2)}, u32[]{:S(2)}) collective-permute-start(bf16[2,20,6,768]{3,2,1,0:T(8,128)(2,1)} %get-tuple-element.64), channel_id=1, source_target_pairs={{1,0},{2,1},{3,2},{4,3},{5,4},{6,5},{7,6},{8,7},{9,8},{10,9},{11,1... | collective-permute-start | bytes 1105928 | tf_op jit(solution)/shard_map/ppermute | solution.py:26
  46.8 2.4 collective-permute-start.2
  49.4 0.9 copy.44
  50.4 0.9 copy.39
  51.5 3.3 collective-permute-done.2
  54.8 2.2 pad_maximum_fusion
  57.0 1.6 fusion.71
  58.6 2.1 squeeze.18
  60.7 3.0 copy.37
  63.7 2.1 squeeze.19
  65.8 2.4 copy.35
  69.2 1.5 fusion.78
  70.8 4.0 %select_convert_fusion = (bf16[64,12,64]{0,2,1:T(8,128)(2,1)}, f32[64,12,64]{0,2,1:T(8,128)S(1)}) fusion(pred[64]{0:T(512)(128)(4,1)S(1)} %broadcast_in_dim.85, bf16[448,12,64]{0,2,1:T(8,128)(2,1)S(1)} %copy-done.23, f32[12,64]{1,0:T(8,128)S(1)} %get-tuple-element.79, f32[12,64,448]{2,1,0:T(8,128)} %copy-done.11), kind=kOutput, calls=%fused_computation.62 | convolution fusion | flops 45122752 | bytes 2362432 | tf_op jit(solution)/shard_map/hqk,khd->qhd/dot_general | solution.py:186
  74.9 4.5 %convolution_bitcast_fusion.1 = f32[448,12,64]{0,2,1:T(8,128)} fusion(bf16[64,12,64]{0,2,1:T(8,128)(2,1)S(1)} %copy-done.21, pred[64]{0:T(512)(128)(4,1)S(1)} %broadcast_in_dim.85, f32[12,64]{1,0:T(8,128)S(1)} %get-tuple-element.79, f32[12,64,448]{2,1,0:T(8,128)} %copy-done.11), kind=kOutput, calls=%fused_computation.19 | convolution fusion | flops 45122752 | bytes 2853952 | tf_op jit(solution)/shard_map/hqk,qhd->khd/dot_general | solution.py:219
  79.5 2.2 subtract_multiply_fusion
  81.7 1.1 fusion.11
  82.8 1.5 multiply_bitcast_fusion
  84.3 5.5 %reshape.416 = f32[12,4,16,16,28]{4,3,2,1,0:T(8,128)} reshape(f32[12,64,448]{2,1,0:T(8,128)S(1)} %subtract_multiply_fusion) | data formatting | bytes 2752512 | tf_op jit(solution)/shard_map/reshape | solution.py:52
  89.8 3.4 %squeeze.16 = bf16[448,12,64]{2,1,0:T(8,128)(2,1)} reshape(bf16[1,16,28,768]{3,2,1,0:T(8,128)(2,1)} %get-tuple-element.60) | data formatting | bytes 1376256 | tf_op jit(solution)/shard_map/squeeze | solution.py:171
  93.2 2.5 copy.33
  95.7 2.1 squeeze.17
  97.8 2.4 copy.30
  101.1 2.4 fusion.79
  103.5 4.1 %select_convert_fusion.1 = (bf16[64,12,64]{0,2,1:T(8,128)(2,1)}, f32[64,12,64]{0,2,1:T(8,128)S(1)}) fusion(pred[64]{0:T(512)(128)(4,1)S(1)} %broadcast_in_dim.80, bf16[448,12,64]{0,2,1:T(8,128)(2,1)S(1)} %copy.33, f32[12,64]{1,0:T(8,128)S(1)} %get-tuple-element.83, f32[12,64,448]{2,1,0:T(8,128)} %copy-done.10), kind=kOutput, calls=%fused_computation.63 | convolution fusion | flops 45122752 | bytes 2362432 | tf_op jit(solution)/shard_map/hqk,khd->qhd/dot_general | solution.py:186
  107.6 4.7 %convolution_bitcast_fusion.2 = f32[448,12,64]{0,2,1:T(8,128)} fusion(bf16[64,12,64]{0,2,1:T(8,128)(2,1)S(1)} %copy-done.20, pred[64]{0:T(512)(128)(4,1)S(1)} %broadcast_in_dim.80, f32[12,64]{1,0:T(8,128)S(1)} %get-tuple-element.83, f32[12,64,448]{2,1,0:T(8,128)} %copy-done.10), kind=kOutput, calls=%fused_computation.20 | convolution fusion | flops 45122752 | bytes 2853952 | tf_op jit(solution)/shard_map/hqk,qhd->khd/dot_general | solution.py:219
  112.4 1.7 subtract_multiply_fusion.1
  114.4 0.8 copy-done.3
  115.2 5.5 %reshape.415 = f32[12,4,16,16,28]{4,3,2,1,0:T(8,128)} reshape(f32[12,64,448]{2,1,0:T(8,128)S(1)} %subtract_multiply_fusion.1) | data formatting | bytes 2752512 | tf_op jit(solution)/shard_map/reshape | solution.py:52
  120.7 3.7 %copy.54 = f32[448,12,64]{2,1,0:T(8,128)} copy(f32[448,12,64]{0,2,1:T(8,128)} %convolution_bitcast_fusion.1) | data formatting | bytes 2752512 | tf_op jit(solution)/shard_map/hqk,qhd->khd/transpose | solution.py:219
  124.3 4.1 %stack.34 = f32[1,16,28,768]{3,2,1,0:T(8,128)} reshape(f32[448,12,64]{2,1,0:T(8,128)} %copy.54) | data formatting | bytes 2752512 | tf_op jit(solution)/shard_map/stack | solution.py:222
  128.4 2.6 copy.53
  131.0 4.1 %stack.33 = f32[1,16,28,768]{3,2,1,0:T(8,128)} reshape(f32[448,12,64]{2,1,0:T(8,128)} %copy.53) | data formatting | bytes 2752512 | tf_op jit(solution)/shard_map/stack | solution.py:222
  135.1 2.6 copy.51
  137.6 3.9 %stack.31 = f32[1,16,28,768]{3,2,1,0:T(8,128)} reshape(f32[448,12,64]{2,1,0:T(8,128)} %copy.51) | data formatting | bytes 2752512 | tf_op jit(solution)/shard_map/stack | solution.py:222
  141.6 2.6 copy.50
  144.2 4.1 %stack.30 = f32[1,16,28,768]{3,2,1,0:T(8,128)} reshape(f32[448,12,64]{2,1,0:T(8,128)} %copy.50) | data formatting | bytes 2752512 | tf_op jit(solution)/shard_map/stack | solution.py:222
  148.2 3.4 %fusion.68 = (bf16[2,20,28,768]{3,2,1,0:T(8,128)(2,1)S(1)}, f32[2,20,28,768]{3,2,1,0:T(8,128)S(1)}) fusion(f32[1,16,28,768]{3,2,1,0:T(8,128)} %stack.34, f32[1,16,28,768]{3,2,1,0:T(8,128)} %stack.33, f32[1,16,28,768]{3,2,1,0:T(8,128)} %stack.31, f32[1,16,28,768]{3,2,1,0:T(8,128)} %stack.30), kind=kLoop, calls=%fused_computation.128 | loop fusion | flops 8601600 | bytes 10665984 | tf_op jit(solution)/shard_map/convert.5
  151.6 1.5 slice.254
  153.2 0.9 fusion.70
  154.1 4.4 %collective-permute-start.4 = (bf16[2,20,6,768]{3,2,1,0:T(8,128)(2,1)S(1)}, bf16[2,20,6,768]{3,2,1,0:T(8,128)(2,1)S(1)}, u32[]{:S(2)}, u32[]{:S(2)}) collective-permute-start(bf16[2,20,6,768]{3,2,1,0:T(8,128)(2,1)S(1)} %get-tuple-element.56), channel_id=1, source_target_pairs={{0,1},{1,2},{2,3},{3,4},{4,5},{5,6},{6,7},{7,8},{8,9},{9,10},{10,1... | collective-permute-start | bytes 1105928 | tf_op jit(solution)/shard_map/ppermute | solution.py:15
  158.4 2.1 collective-permute-start.5
  160.6 3.1 convolution_bitcast_fusion.3
  163.8 3.1 convolution_bitcast_fusion.4
  166.9 1.0 fusion.12
  168.5 1.0 copy-done.2
  169.5 8.1 %scatter-add.14 = f32[2,20,16,768]{3,2,1,0:T(8,128)S(1)} dynamic-update-slice(f32[2,20,16,768]{3,2,1,0:T(8,128)S(1)} %copy-done.2, f32[2,20,6,768]{3,2,1,0:T(8,128)S(1)} %slice_add_fusion.1, s32[]{:T(128)} %constant.171.clone.1, s32[]{:T(128)} %constant.171.clone.1, s32[]{:T(128)} %constant.171.clone.1, s32[]{:T(128)} %constant.171.clone.1) | dynamic-update-slice | bytes 1474564 | tf_op jit(solution)/shard_map/scatter-add | solution.py:103
  177.6 1.2 slice_add_fusion
  178.8 5.0 %scatter-add.15 = f32[2,20,16,768]{3,2,1,0:T(8,128)S(1)} dynamic-update-slice(f32[2,20,16,768]{3,2,1,0:T(8,128)S(1)} %scatter-add.14, f32[2,20,6,768]{3,2,1,0:T(8,128)S(1)} %slice_add_fusion, s32[]{:T(128)} %constant.171.clone.1, s32[]{:T(128)} %constant.171.clone.1, s32[]{:T(128)} %constant.185.clone.1, s32[]{:T(128)} %constant.171.clone.1) | dynamic-update-slice | bytes 1474564 | tf_op jit(solution)/shard_map/scatter-add | solution.py:105
  184.0 0.9 fusion.72
  184.9 2.5 collective-permute-start.6
  188.1 1.2 copy.34
  191.1 1.3 collective-permute-start.7
  193.1 134.7 %psum.7 = f32[12,13,13]{2,1,0:T(8,128)} all-reduce(f32[12,13,13]{2,1,0:T(8,128)S(1)} %fusion.14), channel_id=1, replica_groups=mesh['row'=32,'col'=32] {'row','col'}, use_global_device_ids=true, to_apply=%region_8.9 | all-reduce | flops 2028 | bytes 16224 | tf_op jit(solution)/shard_map/psum | solution.py:247
  327.8 1.0 fusion.20
  (121 shorter events, 10.4 us)
Async XLA Ops:
  0.6 10.8 %copy-start = (f32[12,13,13]{2,1,0:T(8,128)S(1)}, f32[12,13,13]{2,1,0:T(8,128)}, u32[]{:S(2)}) copy-start(f32[12,13,13]{2,1,0:T(8,128)} %param.19) | copy-start | bytes 24340
  2.7 27.6 %collective-permute-start.1 = (bf16[2,6,16,768]{3,2,1,0:T(8,128)(2,1)}, bf16[2,6,16,768]{3,2,1,0:T(8,128)(2,1)S(1)}, u32[]{:S(2)}, u32[]{:S(2)}) collective-permute-start(bf16[2,6,16,768]{3,2,1,0:T(8,128)(2,1)} %get-tuple-element.68), channel_id=1, source_target_pairs={{32,0},{64,32},{96,64},{128,96},{160,128},{192,160},{224,192},{256... | collective-permute-start | bytes 884744 | tf_op jit(solution)/shard_map/ppermute | solution.py:26
  4.0 26.4 %collective-permute-start = (bf16[2,6,16,768]{3,2,1,0:T(8,128)(2,1)}, bf16[2,6,16,768]{3,2,1,0:T(8,128)(2,1)S(1)}, u32[]{:S(2)}, u32[]{:S(2)}) collective-permute-start(bf16[2,6,16,768]{3,2,1,0:T(8,128)(2,1)} %get-tuple-element.67), channel_id=1, source_target_pairs={{0,32},{32,64},{64,96},{96,128},{128,160},{160,192},{192,224},{224... | collective-permute-start | bytes 884744 | tf_op jit(solution)/shard_map/ppermute | solution.py:25
  11.8 4.5 %copy-start.26 = (bf16[8,16,768]{2,1,0:T(8,128)(2,1)S(1)}, bf16[8,16,768]{2,1,0:T(8,128)(2,1)}, u32[]{:S(2)}) copy-start(bf16[8,16,768]{2,1,0:T(8,128)(2,1)} %param.14) | copy-start | bytes 589828
  28.3 2.1 copy-start.15
  28.3 2.1 copy-start.16
  30.4 18.8 %copy-start.27 = (bf16[8,16,768]{2,1,0:T(8,128)(2,1)S(1)}, bf16[8,16,768]{2,1,0:T(8,128)(2,1)}, u32[]{:S(2)}) copy-start(bf16[8,16,768]{2,1,0:T(8,128)(2,1)} %param.17) | copy-start | bytes 589828
  31.6 19.9 %collective-permute-start.3 = (bf16[2,20,6,768]{3,2,1,0:T(8,128)(2,1)}, bf16[2,20,6,768]{3,2,1,0:T(8,128)(2,1)}, u32[]{:S(2)}, u32[]{:S(2)}) collective-permute-start(bf16[2,20,6,768]{3,2,1,0:T(8,128)(2,1)} %get-tuple-element.64), channel_id=1, source_target_pairs={{1,0},{2,1},{3,2},{4,3},{5,4},{6,5},{7,6},{8,7},{9,8},{10,9},{11,1... | collective-permute-start | bytes 1105928 | tf_op jit(solution)/shard_map/ppermute | solution.py:26
  46.8 8.0 %collective-permute-start.2 = (bf16[2,20,6,768]{3,2,1,0:T(8,128)(2,1)}, bf16[2,20,6,768]{3,2,1,0:T(8,128)(2,1)}, u32[]{:S(2)}, u32[]{:S(2)}) collective-permute-start(bf16[2,20,6,768]{3,2,1,0:T(8,128)(2,1)} %get-tuple-element.63), channel_id=1, source_target_pairs={{0,1},{1,2},{2,3},{3,4},{4,5},{5,6},{6,7},{7,8},{8,9},{9,10},{10,1... | collective-permute-start | bytes 1105928 | tf_op jit(solution)/shard_map/ppermute | solution.py:25
  65.8 2.5 copy-start.13
  68.3 0.9 copy-start.7
  69.2 1.7 copy-start.11
  69.2 1.7 copy-start.23
  70.8 4.0 %copy-start.21 = (bf16[64,12,64]{0,2,1:T(8,128)(2,1)S(1)}, bf16[64,12,64]{0,2,1:T(8,128)(2,1)}, u32[]{:S(2)}) copy-start(bf16[64,12,64]{0,2,1:T(8,128)(2,1)} %copy.44) | copy-start | bytes 294916
  79.5 2.2 copy-start.8
  81.7 1.1 copy-start.14
  93.2 2.5 copy-start.12
  95.6 7.9 %copy-start.22 = (bf16[448,12,64]{0,2,1:T(8,128)(2,1)}, bf16[448,12,64]{0,2,1:T(8,128)(2,1)S(1)}, u32[]{:S(2)}) copy-start(bf16[448,12,64]{0,2,1:T(8,128)(2,1)S(1)} %copy.33) | copy-start | bytes 2064388
  100.2 0.9 copy-start.5
  101.1 2.4 copy-start.10
  103.5 4.1 %copy-start.20 = (bf16[64,12,64]{0,2,1:T(8,128)(2,1)S(1)}, bf16[64,12,64]{0,2,1:T(8,128)(2,1)}, u32[]{:S(2)}) copy-start(bf16[64,12,64]{0,2,1:T(8,128)(2,1)} %copy.39) | copy-start | bytes 294916
  114.1 1.2 copy-start.3
  124.3 4.1 %copy-start.9 = (f32[448,12,64]{0,2,1:T(8,128)S(1)}, f32[448,12,64]{0,2,1:T(8,128)}, u32[]{:S(2)}) copy-start(f32[448,12,64]{0,2,1:T(8,128)} %multiply_bitcast_fusion) | copy-start | bytes 4128772
  131.0 4.1 %copy-start.17 = (f32[448,12,64]{0,2,1:T(8,128)S(1)}, f32[448,12,64]{0,2,1:T(8,128)}, u32[]{:S(2)}) copy-start(f32[448,12,64]{0,2,1:T(8,128)} %convolution_bitcast_fusion.2) | copy-start | bytes 4128772
  144.2 16.4 %slice-start = ((s8[6291456]{0:T(1024)(128)(4,1)}), s8[2097152]{0:T(1024)(128)(4,1)S(1)}, s32[]{:S(2)}) async-start(s8[6291456]{0:T(1024)(128)(4,1)} %bitcast.109), calls=%async_computation | async-start | bytes 4194304
  148.2 12.4 %slice-start.1 = ((s8[6291456]{0:T(1024)(128)(4,1)}), s8[4194304]{0:T(1024)(128)(4,1)S(1)}, s32[]{:S(2)}) async-start(s8[6291456]{0:T(1024)(128)(4,1)} %bitcast.109), calls=%async_computation.1 | async-start | bytes 8388608
  148.2 15.5 %slice-start.2 = ((s8[6291456]{0:T(1024)(128)(4,1)}), s8[4194304]{0:T(1024)(128)(4,1)S(1)}, s32[]{:S(2)}) async-start(s8[6291456]{0:T(1024)(128)(4,1)} %bitcast.111), calls=%async_computation.2 | async-start | bytes 8388608
  151.6 12.1 %slice-start.3 = ((s8[6291456]{0:T(1024)(128)(4,1)}), s8[2097152]{0:T(1024)(128)(4,1)S(1)}, s32[]{:S(2)}) async-start(s8[6291456]{0:T(1024)(128)(4,1)} %bitcast.111), calls=%async_computation.3 | async-start | bytes 4194304
  154.1 14.3 %collective-permute-start.4 = (bf16[2,20,6,768]{3,2,1,0:T(8,128)(2,1)S(1)}, bf16[2,20,6,768]{3,2,1,0:T(8,128)(2,1)S(1)}, u32[]{:S(2)}, u32[]{:S(2)}) collective-permute-start(bf16[2,20,6,768]{3,2,1,0:T(8,128)(2,1)S(1)} %get-tuple-element.56), channel_id=1, source_target_pairs={{0,1},{1,2},{2,3},{3,4},{4,5},{5,6},{6,7},{7,8},{8,9},{9,10},{10,1... | collective-permute-start | bytes 1105928 | tf_op jit(solution)/shard_map/ppermute | solution.py:15
  158.4 19.2 %collective-permute-start.5 = (bf16[2,20,6,768]{3,2,1,0:T(8,128)(2,1)}, bf16[2,20,6,768]{3,2,1,0:T(8,128)(2,1)}, u32[]{:S(2)}, u32[]{:S(2)}) collective-permute-start(bf16[2,20,6,768]{3,2,1,0:T(8,128)(2,1)} %get-tuple-element.55), channel_id=1, source_target_pairs={{1,0},{2,1},{3,2},{4,3},{5,4},{6,5},{7,6},{8,7},{9,8},{10,9},{11,1... | collective-permute-start | bytes 1105928 | tf_op jit(solution)/shard_map/ppermute | solution.py:15
  163.8 3.1 copy-start.4
  163.8 3.1 copy-start.6
  168.0 1.5 copy-start.2
  184.0 3.7 %copy-start.25 = (bf16[64,12,64]{0,2,1:T(8,128)(2,1)S(1)}, bf16[64,12,64]{0,2,1:T(8,128)(2,1)}, u32[]{:S(2)}) copy-start(bf16[64,12,64]{0,2,1:T(8,128)(2,1)} %get-tuple-element.81) | copy-start | bytes 294916
  184.0 5.5 %copy-start.18 = (bf16[64,12,64]{0,2,1:T(8,128)(2,1)S(1)}, bf16[64,12,64]{0,2,1:T(8,128)(2,1)}, u32[]{:S(2)}) copy-start(bf16[64,12,64]{0,2,1:T(8,128)(2,1)} %fusion.11) | copy-start | bytes 294916
  184.9 5.1 %copy-start.19 = (bf16[64,12,64]{0,2,1:T(8,128)(2,1)S(1)}, bf16[64,12,64]{0,2,1:T(8,128)(2,1)}, u32[]{:S(2)}) copy-start(bf16[64,12,64]{0,2,1:T(8,128)(2,1)} %fusion.12) | copy-start | bytes 294916
  184.9 142.9 %collective-permute-start.6 = (bf16[2,6,16,768]{3,2,1,0:T(8,128)(2,1)}, bf16[2,6,16,768]{3,2,1,0:T(8,128)(2,1)}, u32[]{:S(2)}, u32[]{:S(2)}) collective-permute-start(bf16[2,6,16,768]{3,2,1,0:T(8,128)(2,1)} %get-tuple-element.62), channel_id=1, source_target_pairs={{0,32},{32,64},{64,96},{96,128},{128,160},{160,192},{192,224},{224... | collective-permute-start | bytes 884744 | tf_op jit(solution)/shard_map/ppermute | solution.py:15
  188.0 3.1 copy-start.24
  191.1 137.8 %collective-permute-start.7 = (bf16[2,6,16,768]{3,2,1,0:T(8,128)(2,1)S(1)}, bf16[2,6,16,768]{3,2,1,0:T(8,128)(2,1)S(1)}, u32[]{:S(2)}, u32[]{:S(2)}) collective-permute-start(bf16[2,6,16,768]{3,2,1,0:T(8,128)(2,1)S(1)} %copy-done.24), channel_id=1, source_target_pairs={{32,0},{64,32},{96,64},{128,96},{160,128},{192,160},{224,192},{256... | collective-permute-start | bytes 884744 | tf_op jit(solution)/shard_map/ppermute | solution.py:15
  327.8 2.0 copy-start.1
where the time goes:
time: 335 us; the launch traced here: 330 us
  blocking collectives  135 us (40%)
  local copies, waits for them, and re-layouts  99.7 us (30%)
  matrix products  40 us (12%)
  starting transfers between devices  34.5 us (10%)
  other arithmetic  16.2 us (5%)
    psum x1, blocking collectives, shards(): d_rel_bias = lax.psum(bias_grad, ('row', 'col'))  135 us
    ppermute x2, starting transfers between devices, with_halo(): after = lax.ppermute(initial, axis, down)  16.4 us
    another operation x4, local copies, waits for them, and re-layouts, group_pass(): jnp.stack([dk_block, dv_block]).reshape(2, band_rows, band_cols, channels)  16.1 us
    squeeze x4, local copies, waits for them, and re-layouts, group_pass(): value_heads = band[1]  11 us
    reshape x2, local copies, waits for them, and re-layouts, offset_sum(): dscore.reshape(head_count, group_rows, tile_cols, band_rows, band_cols)  10.9 us
    ppermute x4, starting transfers between devices, from_behind(): lax.ppermute(value, axis, [(source, source + steps) for source in range(i...  10.3 us
    dot_general x2, matrix products, group_pass(): jnp.einsum('hqk,qhd->khd', prob_b, grad_heads, preferred_element_type=jnp...  9.23 us
    squeeze x4, local copies, waits for them, and re-layouts, group_pass(): key_heads = band[0]  9.06 us
  transfers between devices with their start and end apart: 8, of which 1 were waited for; matrix products, arithmetic and copies ran while one was open for 13% of the time, Pallas kernels for 0%

commit v1 on v0

v1 whole, which is shorter than its diff:
```python
import functools

import jax
import jax.numpy as jnp
from jax import lax
from jax.experimental import pallas as pl
from jax.experimental.pallas import tpu as pltpu
from jax.sharding import PartitionSpec as P

NEG = -1e30
HIGH = lax.Precision.HIGHEST
NT = (((1,), (1,)), ((), ()))
TN = (((0,), (0,)), ((), ()))
NN = (((1,), (0,)), ((), ()))

ROWS = 20
SLOTS = 32
OWN = 16
EDGE = 8
RAD = 6
SPAN = 13
TILE = 128


def dot(a, b, dims, precision=None):
    return lax.dot_general(a, b, dims, precision=precision, preferred_element_type=jnp.float32)


def iota(shape, dim):
    return lax.broadcasted_iota(jnp.int32, shape, dim)


def slot_offset():
    slot = iota((SLOTS, TILE), 0)
    lane = iota((SLOTS, TILE), 1)
    column = jnp.where(
        slot < OWN, slot + RAD, jnp.where(slot < OWN + EDGE, slot - OWN - EDGE + RAD, slot - EDGE + RAD)
    )
    return column - (lane & 15), lane >> 4


def row_pick(dim):
    shape = (16, 2 * TILE)
    lane = iota(shape, 1)
    offset = ((8 - ((lane >> 4) & 7)) & 7) + 8 * (lane >> 7)
    return (iota(shape, 0) == offset).astype(jnp.float32)


def bias_body(ext_ref, table_ref, out_ref, mask_ref):
    offset, query_row = slot_offset()

    @pl.when(pl.program_id(0) == 0)
    def _():
        row, col = lax.axis_index("row"), lax.axis_index("col")
        last_row, last_col = ext_ref.shape[1] - 1, ext_ref.shape[2] - 1
        slot = iota((SLOTS, TILE), 0)
        lane = iota((SLOTS, TILE), 1)
        panel = row // 2
        valid_query = ((row % 2) * 8 + query_row < ext_ref[0, panel, col]) & (
            (lane & 15) < ext_ref[1, panel, col]
        )
        near = valid_query & (offset >= 0) & (offset < SPAN)
        local = jnp.where(slot < OWN, slot, jnp.where(slot < OWN + EDGE, slot - EDGE, slot - OWN - EDGE))
        for j in range(ROWS):
            r = row * 8 + (j - RAD + 16)
            panel_row = r // 16 - 1
            inside_row = (panel_row >= 0) & (panel_row <= last_row)
            panel_row = jnp.minimum(jnp.maximum(panel_row, 0), last_row)
            widths = []
            for step in (0, -1, 1):
                at = col + step
                inside = inside_row & (at >= 0) & (at <= last_col)
                at = jnp.minimum(jnp.maximum(at, 0), last_col)
                tall = inside & (r % 16 < ext_ref[0, panel_row, at])
                widths.append(jnp.where(tall, ext_ref[1, panel_row, at], 0))
            width = jnp.where(slot < OWN, widths[0], jnp.where(slot < OWN + EDGE, widths[1], widths[2]))
            allowed = near & (local < width) & (query_row <= j) & (query_row >= j - SPAN + 1)
            mask_ref[j * SLOTS : (j + 1) * SLOTS, :] = jnp.where(allowed, 0.0, NEG)

    spread = dot(table_ref[0], row_pick(0), NN, HIGH)
    low = jnp.zeros((SLOTS, TILE), jnp.float32)
    high = jnp.zeros((SLOTS, TILE), jnp.float32)
    for b in range(SPAN):
        low = jnp.where(offset == b, spread[b : b + 1, :TILE], low)
        high = jnp.where(offset == b, spread[b : b + 1, TILE:], high)
    for turn in range(8):
        low_turned = pltpu.roll(low, 16 * turn, 1) if turn else low
        high_turned = pltpu.roll(high, 16 * turn, 1) if turn else high
        for j in (turn, turn + 8, turn + 16):
            if j >= ROWS:
                continue
            value = low_turned if j < 8 else high_turned
            if 8 <= j < 15:
                value = jnp.where(query_row > j - 8, low_turned, high_turned)
            at = slice(j * SLOTS, (j + 1) * SLOTS)
            out_ref[0, at, :] = value + mask_ref[at, :]


def attend_body(
    ext_ref, bias_ref, q_ref, g_ref, k_ref, v_ref, t_ref, b_ref, l_ref, r_ref, lc_ref, rc_ref,
    out_ref, dq_ref, own_ref, top_ref, bottom_ref, left_ref, right_ref, part_ref,
    kw_ref, vw_ref, sum_ref,
):
    pair = pl.program_id(0)
    for n, (own, window) in enumerate(((k_ref, kw_ref), (v_ref, vw_ref))):
        window[0:6, 0:16] = t_ref[n]
        window[6:14, 0:16] = own[...]
        window[14:20, 0:16] = b_ref[n]
        window[0:6, 16:24] = lc_ref[n, 0:6]
        window[6:14, 16:24] = l_ref[n]
        window[14:20, 16:24] = lc_ref[n, 6:12]
        window[0:6, 24:32] = rc_ref[n, 0:6]
        window[6:14, 24:32] = r_ref[n]
        window[14:20, 24:32] = rc_ref[n, 6:12]
    keys = kw_ref[...].reshape(ROWS * SLOTS, TILE)
    values = vw_ref[...].reshape(ROWS * SLOTS, TILE)

    row, col = lax.axis_index("row"), lax.axis_index("col")
    panel = row // 2
    token = iota((TILE, TILE), 0)
    valid = ((row % 2) * 8 + (token >> 4) < ext_ref[0, panel, col]) & (
        (token & 15) < ext_ref[1, panel, col]
    )
    first = iota((TILE, TILE), 1) < 64
    queries = q_ref[...].reshape(TILE, TILE).astype(jnp.float32) * 0.125
    grads = jnp.where(valid, g_ref[...].reshape(TILE, TILE).astype(jnp.float32), 0.0)

    def apart(x):
        return jnp.concatenate([jnp.where(first, x, 0.0), jnp.where(first, 0.0, x)], 0)

    grads_f = apart(grads)
    queries_b = apart(queries).astype(jnp.bfloat16)
    grads_b = grads_f.astype(jnp.bfloat16)

    score = dot(keys, queries_b, NT)
    score = score + jnp.concatenate([bias_ref[0], bias_ref[1]], 1)
    highest = jnp.max(score, axis=0, keepdims=True)
    weights = jnp.exp(score - highest)
    prob = weights * (1.0 / jnp.sum(weights, axis=0, keepdims=True))
    prob_b = prob.astype(jnp.bfloat16)
    output = dot(values, prob_b, TN)
    delta = jnp.sum(jnp.transpose(grads_f) * output, axis=0, keepdims=True)
    dprob = dot(values, grads_b, NT)
    dscore = prob * (dprob - delta)
    dscore_b = dscore.astype(jnp.bfloat16)

    head_row = iota((TILE, TILE), 0) < 64

    def together(x):
        return jnp.transpose(jnp.where(head_row, x[:, :TILE], x[:, TILE:]))

    attended = jnp.where(valid, together(output), 0.0)
    out_ref[...] = attended.astype(jnp.bfloat16).reshape(8, 16, TILE)
    dq = together(dot(keys, dscore_b, TN)) * 0.125
    dq_ref[...] = dq.astype(jnp.bfloat16).reshape(8, 16, TILE)
    dk = dot(dscore_b, queries_b, NN)
    dv = dot(prob_b, grads_b, NN)
    for n, grad in enumerate((dk, dv)):
        grad = grad.reshape(ROWS, SLOTS, TILE)
        top_ref[n] = grad[0:6, 0:16]
        own_ref[n] = grad[6:14, 0:16]
        bottom_ref[n] = grad[14:20, 0:16]
        left_ref[n] = grad[:, 16:24].astype(jnp.bfloat16)
        right_ref[n] = grad[:, 24:32].astype(jnp.bfloat16)

    @pl.when(pair == 0)
    def _():
        sum_ref[...] = jnp.zeros_like(sum_ref)

    offset, query_row = slot_offset()
    for head in range(2):
        part = dscore[:, head * TILE : (head + 1) * TILE]
        low = jnp.zeros((SLOTS, TILE), jnp.float32)
        high = jnp.zeros((SLOTS, TILE), jnp.float32)

        def line(j, part=part):
            return part[j * SLOTS : (j + 1) * SLOTS]

        for turn in range(8):
            x = line(turn)
            y = line(turn + 8)
            if turn < 7:
                x = x + jnp.where(query_row > turn, y, 0.0)
                y = jnp.where(query_row > turn, 0.0, y)
            if turn + 16 < ROWS:
                y = y + line(turn + 16)
            back = (TILE - 16 * turn) % TILE
            low = low + (pltpu.roll(x, back, 1) if turn else x)
            high = high + (pltpu.roll(y, back, 1) if turn else y)
        for b in range(SPAN):
            hit = offset == b
            sum_ref[2 * pair + head, b : b + 1, :TILE] = jnp.sum(
                jnp.where(hit, low, 0.0), axis=0, keepdims=True
            )
            sum_ref[2 * pair + head, b : b + 1, TILE:] = jnp.sum(
                jnp.where(hit, high, 0.0), axis=0, keepdims=True
            )

    @pl.when(pair == pl.num_programs(0) - 1)
    def _():
        pick = row_pick(0)
        for half in range(2):
            sums = sum_ref[half * 8 : half * 8 + 8].reshape(TILE, 2 * TILE)
            part_ref[half * 16 : half * 16 + 16, :] = dot(pick, sums, NT, HIGH)


def border_body(top_ref, bottom_ref, fl_ref, fr_ref, up_ref, down_ref):
    for source, rows, target in ((top_ref, slice(0, 6), up_ref), (bottom_ref, slice(14, 20), down_ref)):
        for n in range(2):
            low = source[n, :, :EDGE] + fl_ref[n, rows].astype(jnp.float32)
            high = source[n, :, EDGE:] + fr_ref[n, rows].astype(jnp.float32)
            target[n] = jnp.concatenate([low, high], 1).astype(jnp.bfloat16)


def final_body(own_ref, fl_ref, fr_ref, fu_ref, fd_ref, part_ref, dk_ref, dv_ref, bias_ref):
    for n, target in enumerate((dk_ref, dv_ref)):
        for r in range(8):
            left = own_ref[n, r, :EDGE] + fl_ref[n, r + RAD].astype(jnp.float32)
            right = own_ref[n, r, EDGE:] + fr_ref[n, r + RAD].astype(jnp.float32)
            total = jnp.concatenate([left, right], 0)
            if r < RAD:
                total = total + fu_ref[n, r].astype(jnp.float32)
            if r >= 8 - RAD:
                total = total + fd_ref[n, r - 8 + RAD].astype(jnp.float32)
            target[r] = total.astype(jnp.bfloat16)
    for h in range(bias_ref.shape[0]):
        at = (h % 8) * 16
        bias_ref[h] = part_ref[(h // 8) * 16 : (h // 8) * 16 + SPAN, at : at + SPAN]


def neighbour(value, axis, step):
    size = lax.axis_size(axis)
    return lax.ppermute(value, axis, [(i, i + step) for i in range(size) if 0 <= i + step < size])


def exchange(value, axis):
    return lax.all_to_all(value, axis, 0, 0)


def gathered(piece, axis):
    return exchange(jnp.broadcast_to(piece, (lax.axis_size(axis),) + piece.shape), axis)


def shape(dims, dtype=jnp.bfloat16):
    return jax.ShapeDtypeStruct(dims, dtype)


SMEM = pl.BlockSpec(memory_space=pltpu.SMEM)
VMEM = pl.BlockSpec(memory_space=pltpu.VMEM)


def shards(queries, keys, values, d_out, extents, rel_bias):
    heads = rel_bias.shape[0]
    width = queries.shape[2]
    both = jnp.stack([keys, values])
    top = neighbour(both[:, 2:], "row", 1)
    bottom = neighbour(both[:, :6], "row", -1)
    left = neighbour(both[:, :, EDGE:], "col", 1)
    right = neighbour(both[:, :, :EDGE], "col", -1)

    table = jnp.pad(jnp.swapaxes(rel_bias, 1, 2), ((0, 0), (0, 3), (0, 3)))
    bias = pl.pallas_call(
        bias_body,
        grid=(heads,),
        out_shape=shape((heads, ROWS * SLOTS, TILE), jnp.float32),
        in_specs=[SMEM, pl.BlockSpec((1, 16, 16), lambda h: (h, 0, 0))],
        out_specs=pl.BlockSpec((1, ROWS * SLOTS, TILE), lambda h: (h, 0, 0)),
        scratch_shapes=[pltpu.VMEM((ROWS * SLOTS, TILE), jnp.float32)],
        cost_estimate=pl.CostEstimate(flops=20_000_000, bytes_accessed=4_000_000, transcendentals=0),
        name="bias_mask",
    )(extents, table)

    top, bottom, left, right, bias = lax.optimization_barrier((top, bottom, left, right, bias))
    ends = jnp.concatenate([top, bottom], 1)
    left_ends = neighbour(ends[:, :, EDGE:], "col", 1)
    right_ends = neighbour(ends[:, :, :EDGE], "col", -1)

    def lanes(*dims):
        return pl.BlockSpec(dims + (TILE,), lambda g: (0,) * len(dims) + (g,))

    tile = lanes(8, 16)
    rows_spec, edge_spec, ends_spec = lanes(2, 6, 16), lanes(2, 8, EDGE), lanes(2, 12, EDGE)
    side_spec = lanes(2, ROWS, EDGE)
    attended, d_queries, own, d_top, d_bottom, d_left, d_right, part = pl.pallas_call(
        attend_body,
        grid=(width // TILE,),
        out_shape=(
            shape(queries.shape),
            shape(queries.shape),
            shape((2, 8, 16, width), jnp.float32),
            shape((2, 6, 16, width), jnp.float32),
            shape((2, 6, 16, width), jnp.float32),
            shape((2, ROWS, EDGE, width)),
            shape((2, ROWS, EDGE, width)),
            shape((32, TILE), jnp.float32),
        ),
        in_specs=[
            SMEM,
            pl.BlockSpec((2, ROWS * SLOTS, TILE), lambda g: (g, 0, 0)),
            tile, tile, tile, tile,
            rows_spec, rows_spec, edge_spec, edge_spec, ends_spec, ends_spec,
        ],
        out_specs=(
            tile, tile, lanes(2, 8, 16), rows_spec, rows_spec, side_spec, side_spec,
            pl.BlockSpec((32, TILE), lambda g: (0, 0)),
        ),
        scratch_shapes=[
            pltpu.VMEM((ROWS, SLOTS, TILE), jnp.bfloat16),
            pltpu.VMEM((ROWS, SLOTS, TILE), jnp.bfloat16),
            pltpu.VMEM((16, 16, 2 * TILE), jnp.float32),
        ],
        cost_estimate=pl.CostEstimate(
            flops=1_500_000_000, bytes_accessed=9_000_000, transcendentals=1_000_000
        ),
        name="attend",
    )(extents, bias, queries, d_out, keys, values, top, bottom, left, right, left_ends, right_ends)

    from_left = neighbour(d_right, "col", 1)
    from_right = neighbour(d_left, "col", -1)
    piece = exchange(part.reshape(lax.axis_size("col"), -1, TILE), "col")
    from_left, from_right, piece = lax.optimization_barrier((from_left, from_right, piece))
    up, down = pl.pallas_call(
        border_body,
        out_shape=(shape(d_top.shape), shape(d_top.shape)),
        in_specs=[VMEM] * 4,
        out_specs=(VMEM, VMEM),
        name="border",
    )(d_top, d_bottom, from_left, from_right)
    up, down, piece = lax.optimization_barrier((up, down, piece))
    total = gathered(jnp.sum(gathered(jnp.sum(piece, 0), "row"), 0), "col").reshape(part.shape)
    from_below = neighbour(up, "row", -1)
    from_above = neighbour(down, "row", 1)
    d_keys, d_values, d_rel_bias = pl.pallas_call(
        final_body,
        out_shape=(shape(keys.shape), shape(keys.shape), shape(rel_bias.shape, jnp.float32)),
        in_specs=[VMEM] * 6,
        out_specs=(VMEM, VMEM, VMEM),
        name="final",
    )(own, from_left, from_right, from_above, from_below, total)
    return (attended, d_queries, d_keys, d_values, d_rel_bias)


def solution(mesh):
    tiles = P("row", "col", None)
    return jax.shard_map(
        shards,
        mesh=mesh,
        in_specs=(tiles, tiles, tiles, tiles, P(), P()),
        out_specs=(tiles, tiles, tiles, tiles, P()),
        check_vma=False,
    )
```

time: 335 us -> 138 us (0.41)
  local copies, waits for them, and re-layouts: 99.7 us -> 4.31 us
  blocking collectives: 135 us -> 61 us
  matrix products: 40 us -> 0 us
  Pallas kernels: 0 us -> 25.5 us
  other arithmetic: 16.2 us -> 2.32 us
  starting transfers between devices: 34.5 us -> 38.7 us
    psum x1 -> x0, blocking collectives: 135 us -> none  [shards(): d_rel_bias = lax.psum(bias_grad, ('row', 'col'))]
    all_to_all x0 -> x3, blocking collectives: none -> 61 us  [exchange(): return lax.all_to_all(value, axis, 0, 0)]
    dot_general x22 -> x0, matrix products: 40 us -> none  [the longest x2 9.23 us: group_pass(): jnp.einsum('hqk,qhd->khd', prob_b, grad_heads, preferred_element_type=jnp...]
    pallas_call x0 -> x4, Pallas kernels: none -> 25.5 us  [the longest x1 11.7 us: shards(): pl.pallas_call(attend_body, grid=(width // TILE,), out_shape=(shape(queri...]
    reshape x15 -> x0, local copies, waits for them, and re-layouts: 20.3 us -> none  [the longest x2 10.9 us: offset_sum(): dscore.reshape(head_count, group_rows, tile_cols, band_rows, band_cols)]
    squeeze x8 -> x0, local copies, waits for them, and re-layouts: 20 us -> none  [the longest x4 11 us: group_pass(): value_heads = band[1]]
    another operation x4 -> x0, local copies, waits for them, and re-layouts: 16.1 us -> none  [group_pass(): jnp.stack([dk_block, dv_block]).reshape(2, band_rows, band_cols, channels)]
    scatter-add x2 -> x0, local copies, waits for them, and re-layouts: 13.1 us -> none  [the longest x1 8.11 us: fold_cols(): interior = interior.at[:, :, :radius].add(arrived)]
  transfers between devices with their start and end apart: 8 -> 10, of which waited for: 1 -> 2; matrix products, arithmetic and copies ran while one was open for 13% -> 2% of each run, Pallas kernels for 0% -> 6%
where the time goes in v1:
time: 138 us; the launch traced here: 136 us
  blocking collectives  61 us (44%)
  starting transfers between devices  38.7 us (28%)
  Pallas kernels  25.5 us (18%)
  local copies, waits for them, and re-layouts  4.31 us (3%)
  waiting for transfers between devices  3.66 us (3%)
  other arithmetic  2.32 us (2%)
    all_to_all x3, blocking collectives, exchange(): return lax.all_to_all(value, axis, 0, 0)  61 us
    ppermute x10, starting transfers between devices, neighbour(): lax.ppermute(value, axis, [(i, i + step) for i in range(size) if 0 <= i +...  38.7 us
    pallas_call x1, Pallas kernels, shards(): pl.pallas_call(attend_body, grid=(width // TILE,), out_shape=(shape(queri...  11.7 us
    pallas_call x1, Pallas kernels, shards(): pl.pallas_call(bias_body, grid=(heads,), out_shape=shape((heads, ROWS * S...  8.86 us
    ppermute x10, waiting for transfers between devices, neighbour(): lax.ppermute(value, axis, [(i, i + step) for i in range(size) if 0 <= i +...  3.66 us
    unnamed x22, local copies, waits for them, and re-layouts  3.57 us
  transfers between devices with their start and end apart: 10, of which 2 were waited for; matrix products, arithmetic and copies ran while one was open for 2% of the time, Pallas kernels for 6%

profile of v1, /device:TPU:1, one launch (start us, length us, event | category | flops | bytes accessed | tf_op | source)
XLA Modules:
  0.0 136.4 jit_solution(10553383098564360665)
XLA Ops:
  0.6 1.2 fusion.1
  1.8 1.3 collective-permute-start.1
  3.1 5.5 %collective-permute-start = (bf16[2,6,16,768]{3,2,1,0:T(8,128)(2,1)S(1)}, bf16[2,6,16,768]{3,2,1,0:T(8,128)(2,1)S(1)}, u32[]{:S(2)}, u32[]{:S(2)}) collective-permute-start(bf16[2,6,16,768]{3,2,1,0:T(8,128)(2,1)S(1)} %get-tuple-element.58), channel_id=1, source_target_pairs={{0,32},{32,64},{64,96},{96,128},{128,160},{160,192},{192,224},{224... | collective-permute-start | bytes 884744 | tf_op jit(solution)/shard_map/ppermute | solution.py:233
  8.6 1.1 pad_maximum_fusion
  9.7 15.2 %collective-permute-start.3 = (bf16[2,8,8,768]{3,2,1,0:T(8,128)(2,1)S(1)}, bf16[2,8,8,768]{3,2,1,0:T(8,128)(2,1)S(1)}, u32[]{:S(2)}, u32[]{:S(2)}) collective-permute-start(bf16[2,8,8,768]{3,2,1,0:T(8,128)(2,1)S(1)} %get-tuple-element.55), channel_id=1, source_target_pairs={{1,0},{2,1},{3,2},{4,3},{5,4},{6,5},{7,6},{8,7},{9,8},{10,9},{11,1... | collective-permute-start | bytes 589832 | tf_op jit(solution)/shard_map/ppermute | solution.py:233
  24.8 1.9 %collective-permute-start.2 = (bf16[2,8,8,768]{3,2,1,0:T(8,128)(2,1)S(1)}, bf16[2,8,8,768]{3,2,1,0:T(8,128)(2,1)S(1)}, u32[]{:S(2)}, u32[]{:S(2)}) collective-permute-start(bf16[2,8,8,768]{3,2,1,0:T(8,128)(2,1)S(1)} %get-tuple-element.56), channel_id=1, source_target_pairs={{0,1},{1,2},{2,3},{3,4},{4,5},{5,6},{6,7},{7,8},{8,9},{9,10},{10,1... | collective-permute-start | bytes 589832 | tf_op jit(solution)/shard_map/ppermute | solution.py:233
  26.8 1.0 copy.16
  27.8 0.7 pad.4.table_ref
  28.5 8.9 %bias_mask.1.bias_ref = f32[12,640,128]{2,1,0:T(8,128)} custom-call(s32[2,16,32]{2,1,0:T(8,128)} %ext_ref.3, f32[12,16,16]{2,1,0:T(8,128)} %pad.4.table_ref), custom_call_target="tpu_custom_call" | custom-call | flops 20000000 | bytes 4000000 | tf_op jit(solution)/shard_map/bias_mask/pallas_call | solution.py:262
  37.3 0.0 collective-permute-done.3.r_ref
  37.3 0.0 copy-start.8
  37.3 0.0 collective-permute-done.2.l_ref
  37.3 0.0 copy-start.9
  37.3 0.0 collective-permute-done.1.b_ref
  37.3 0.0 copy-start.2
  37.4 0.0 collective-permute-done.t_ref
  37.4 0.0 copy-start.3
  37.5 2.4 %collective-permute-start.5 = (bf16[2,12,8,768]{3,2,1,0:T(8,128)(2,1)S(1)}, bf16[2,12,8,768]{3,2,1,0:T(8,128)(2,1)S(1)}, u32[]{:S(2)}, u32[]{:S(2)}) collective-permute-start(bf16[2,12,8,768]{3,2,1,0:T(8,128)(2,1)S(1)} %get-tuple-element.53), channel_id=1, source_target_pairs={{1,0},{2,1},{3,2},{4,3},{5,4},{6,5},{7,6},{8,7},{9,8},{10,9},{11,1... | collective-permute-start | bytes 884744 | tf_op jit(solution)/shard_map/ppermute | solution.py:233
  39.9 3.1 %collective-permute-start.4 = (bf16[2,12,8,768]{3,2,1,0:T(8,128)(2,1)S(1)}, bf16[2,12,8,768]{3,2,1,0:T(8,128)(2,1)S(1)}, u32[]{:S(2)}, u32[]{:S(2)}) collective-permute-start(bf16[2,12,8,768]{3,2,1,0:T(8,128)(2,1)S(1)} %get-tuple-element.54), channel_id=1, source_target_pairs={{0,1},{1,2},{2,3},{3,4},{4,5},{5,6},{6,7},{7,8},{8,9},{9,10},{10,1... | collective-permute-start | bytes 884744 | tf_op jit(solution)/shard_map/ppermute | solution.py:233
  43.1 2.5 %collective-permute-done.5.rc_ref = bf16[2,12,8,768]{3,2,1,0:T(8,128)(2,1)S(1)} collective-permute-done((bf16[2,12,8,768]{3,2,1,0:T(8,128)(2,1)S(1)}, bf16[2,12,8,768]{3,2,1,0:T(8,128)(2,1)S(1)}, u32[]{:S(2)}, u32[]{:S(2)}) %collective-permute-start.5) | collective-permute-done | bytes 294944 | tf_op jit(solution)/shard_map/ppermute | solution.py:233
  45.5 0.0 copy-start.6
  45.5 1.2 collective-permute-done.4.lc_ref
  46.7 0.0 copy-done.8
  46.7 0.0 copy-done.9
  46.7 0.0 copy-done.2
  46.7 0.0 copy-done.3
  46.7 0.0 copy-done.6
  46.7 0.0 copy-start.7
  46.7 0.7 copy-done.7
  47.5 11.7 %attend.1 = (bf16[8,16,768]{2,1,0:T(8,128)(2,1)}, bf16[8,16,768]{2,1,0:T(8,128)(2,1)}, f32[2,8,16,768]{3,2,1,0:T(8,128)}, f32[2,6,16,768]{3,2,1,0:T(8,128)}, f32...) custom-call(s32[2,16,32]{2,1,0:T(8,128)} %ext_ref.3, ...), custom_call_target="tpu_custom_call" | custom-call | flops 1500000000 | bytes 9000000 | tf_op jit(solution)/shard_map/attend/pallas_call | solution.py:284
  59.2 4.4 %collective-permute-start.6 = (bf16[2,20,8,768]{3,2,1,0:T(8,128)(2,1)}, bf16[2,20,8,768]{3,2,1,0:T(8,128)(2,1)S(1)}, u32[]{:S(2)}, u32[]{:S(2)}) collective-permute-start(bf16[2,20,8,768]{3,2,1,0:T(8,128)(2,1)} %get-tuple-element.37), channel_id=1, source_target_pairs={{0,1},{1,2},{2,3},{3,4},{4,5},{5,6},{6,7},{7,8},{8,9},{9,10},{10,1... | collective-permute-start | bytes 1474568 | tf_op jit(solution)/shard_map/ppermute | solution.py:233
  63.6 1.9 %collective-permute-start.7 = (bf16[2,20,8,768]{3,2,1,0:T(8,128)(2,1)}, bf16[2,20,8,768]{3,2,1,0:T(8,128)(2,1)S(1)}, u32[]{:S(2)}, u32[]{:S(2)}) collective-permute-start(bf16[2,20,8,768]{3,2,1,0:T(8,128)(2,1)} %get-tuple-element.38), channel_id=1, source_target_pairs={{1,0},{2,1},{3,2},{4,3},{5,4},{6,5},{7,6},{8,7},{9,8},{10,9},{11,1... | collective-permute-start | bytes 1474568 | tf_op jit(solution)/shard_map/ppermute | solution.py:233
  65.5 11.3 %all_to_all.15 = f32[32,1,128]{2,1,0:T(1,128)S(1)} all-to-all(f32[32,1,128]{2,1,0:T(1,128)} %bitcast.15), channel_id=1, replica_groups=mesh['row'=32,'col'=32] {'col'}, dimensions={0} | all-to-all | bytes 32768 | tf_op jit(solution)/shard_map/all_to_all | solution.py:237
  76.9 0.0 collective-permute-done.6.fl_ref
  76.9 0.0 copy-start
  76.9 0.0 collective-permute-done.7.fr_ref
  76.9 0.0 copy-start.1
  76.9 0.8 copy-done
  77.7 0.2 copy-done.1
  77.8 2.4 %border.1 = (bf16[2,6,16,768]{3,2,1,0:T(8,128)(2,1)}, bf16[2,6,16,768]{3,2,1,0:T(8,128)(2,1)}) custom-call(f32[2,6,16,768]{3,2,1,0:T(8,128)} %get-tuple-element.42.top_ref, f32[2,6,16,768]{3,2,1,0:T(8,128)} %get-tuple-element.43.bottom_ref, bf16[2,20,8,768]{3,2,1,0:T(8,128)(2,1)} %copy-done, bf16[2,20,8,768]{3,2,1,0:T(8,128)(2,1)} %copy-done.1), custom_call_target="tpu_custom_call" | custom-call | tf_op jit(solution)/shard_map/border/pallas_call | solution.py:322
  80.3 1.7 %collective-permute-start.8 = (bf16[2,6,16,768]{3,2,1,0:T(8,128)(2,1)}, bf16[2,6,16,768]{3,2,1,0:T(8,128)(2,1)S(1)}, u32[]{:S(2)}, u32[]{:S(2)}) collective-permute-start(bf16[2,6,16,768]{3,2,1,0:T(8,128)(2,1)} %get-tuple-element.47), channel_id=1, source_target_pairs={{0,32},{32,64},{64,96},{96,128},{128,160},{160,192},{192,224},{224... | collective-permute-start | bytes 884744 | tf_op jit(solution)/shard_map/ppermute | solution.py:233
  82.0 1.3 collective-permute-start.9
  83.3 0.1 reduce_sum.18
  83.3 35.9 %all_to_all.16 = f32[32,1,128]{2,1,0:T(1,128)S(1)} all-to-all(f32[32,1,128]{2,1,0:T(1,128)S(1)} %broadcast_in_dim.6), channel_id=1, replica_groups=mesh['row'=32,'col'=32] {'row'}, dimensions={0} | all-to-all | bytes 32768 | tf_op jit(solution)/shard_map/all_to_all | solution.py:237
  119.3 13.8 %all_to_all.17 = f32[32,1,128]{2,1,0:T(1,128)} all-to-all(f32[32,1,128]{2,1,0:T(1,128)S(1)} %broadcast_in_dim.7), channel_id=1, replica_groups=mesh['row'=32,'col'=32] {'col'}, dimensions={0} | all-to-all | bytes 32768 | tf_op jit(solution)/shard_map/all_to_all | solution.py:237
  133.1 0.0 collective-permute-done.8.fu_ref
  133.1 0.0 copy-start.4
  133.1 0.0 collective-permute-done.9.fd_ref
  133.1 0.0 copy-start.5
  133.1 0.7 copy-done.4
  133.8 0.1 copy-done.5
  133.9 2.4 %final.1 = (bf16[8,16,768]{2,1,0:T(8,128)(2,1)}, bf16[8,16,768]{2,1,0:T(8,128)(2,1)}, f32[12,13,13]{2,1,0:T(8,128)}) custom-call(f32[2,8,16,768]{3,2,1,0:T(8,128)} %get-tuple-element.36.own_ref, bf16[2,20,8,768]{3,2,1,0:T(8,128)(2,1)} %copy-done, bf16[2,20,8,768]{3,2,1,0:T(8,128)(2,1)} %copy-done.1, bf16[2,6,16,768]{3,2,1,0:T(8,128)(2,1)} %copy-done.4, ...), custom_call_target="tpu_custom_call" | custom-call | tf_op jit(solution)/shard_map/final/pallas_call | solution.py:333
  (6 shorter events, 0.1 us)
Async XLA Ops:
  1.8 35.5 %collective-permute-start.1 = (bf16[2,6,16,768]{3,2,1,0:T(8,128)(2,1)S(1)}, bf16[2,6,16,768]{3,2,1,0:T(8,128)(2,1)S(1)}, u32[]{:S(2)}, u32[]{:S(2)}) collective-permute-start(bf16[2,6,16,768]{3,2,1,0:T(8,128)(2,1)S(1)} %get-tuple-element.57), channel_id=1, source_target_pairs={{32,0},{64,32},{96,64},{128,96},{160,128},{192,160},{224,192},{256... | collective-permute-start | bytes 884744 | tf_op jit(solution)/shard_map/ppermute | solution.py:233
  3.1 34.2 %collective-permute-start = (bf16[2,6,16,768]{3,2,1,0:T(8,128)(2,1)S(1)}, bf16[2,6,16,768]{3,2,1,0:T(8,128)(2,1)S(1)}, u32[]{:S(2)}, u32[]{:S(2)}) collective-permute-start(bf16[2,6,16,768]{3,2,1,0:T(8,128)(2,1)S(1)} %get-tuple-element.58), channel_id=1, source_target_pairs={{0,32},{32,64},{64,96},{96,128},{128,160},{160,192},{192,224},{224... | collective-permute-start | bytes 884744 | tf_op jit(solution)/shard_map/ppermute | solution.py:233
  9.7 27.7 %collective-permute-start.3 = (bf16[2,8,8,768]{3,2,1,0:T(8,128)(2,1)S(1)}, bf16[2,8,8,768]{3,2,1,0:T(8,128)(2,1)S(1)}, u32[]{:S(2)}, u32[]{:S(2)}) collective-permute-start(bf16[2,8,8,768]{3,2,1,0:T(8,128)(2,1)S(1)} %get-tuple-element.55), channel_id=1, source_target_pairs={{1,0},{2,1},{3,2},{4,3},{5,4},{6,5},{7,6},{8,7},{9,8},{10,9},{11,1... | collective-permute-start | bytes 589832 | tf_op jit(solution)/shard_map/ppermute | solution.py:233
  24.8 12.5 %collective-permute-start.2 = (bf16[2,8,8,768]{3,2,1,0:T(8,128)(2,1)S(1)}, bf16[2,8,8,768]{3,2,1,0:T(8,128)(2,1)S(1)}, u32[]{:S(2)}, u32[]{:S(2)}) collective-permute-start(bf16[2,8,8,768]{3,2,1,0:T(8,128)(2,1)S(1)} %get-tuple-element.56), channel_id=1, source_target_pairs={{0,1},{1,2},{2,3},{3,4},{4,5},{5,6},{6,7},{7,8},{8,9},{9,10},{10,1... | collective-permute-start | bytes 589832 | tf_op jit(solution)/shard_map/ppermute | solution.py:233
  37.3 9.4 %copy-start.8 = (bf16[2,8,8,768]{3,2,1,0:T(8,128)(2,1)}, bf16[2,8,8,768]{3,2,1,0:T(8,128)(2,1)S(1)}, u32[]{:S(2)}) copy-start(bf16[2,8,8,768]{3,2,1,0:T(8,128)(2,1)S(1)} %collective-permute-done.3.r_ref) | copy-start | bytes 589828
  37.3 9.4 %copy-start.9 = (bf16[2,8,8,768]{3,2,1,0:T(8,128)(2,1)}, bf16[2,8,8,768]{3,2,1,0:T(8,128)(2,1)S(1)}, u32[]{:S(2)}) copy-start(bf16[2,8,8,768]{3,2,1,0:T(8,128)(2,1)S(1)} %collective-permute-done.2.l_ref) | copy-start | bytes 589828
  37.3 9.4 %copy-start.2 = (bf16[2,6,16,768]{3,2,1,0:T(8,128)(2,1)}, bf16[2,6,16,768]{3,2,1,0:T(8,128)(2,1)S(1)}, u32[]{:S(2)}) copy-start(bf16[2,6,16,768]{3,2,1,0:T(8,128)(2,1)S(1)} %collective-permute-done.1.b_ref) | copy-start | bytes 884740
  37.4 9.4 %copy-start.3 = (bf16[2,6,16,768]{3,2,1,0:T(8,128)(2,1)}, bf16[2,6,16,768]{3,2,1,0:T(8,128)(2,1)S(1)}, u32[]{:S(2)}) copy-start(bf16[2,6,16,768]{3,2,1,0:T(8,128)(2,1)S(1)} %collective-permute-done.t_ref) | copy-start | bytes 884740
  37.5 8.0 %collective-permute-start.5 = (bf16[2,12,8,768]{3,2,1,0:T(8,128)(2,1)S(1)}, bf16[2,12,8,768]{3,2,1,0:T(8,128)(2,1)S(1)}, u32[]{:S(2)}, u32[]{:S(2)}) collective-permute-start(bf16[2,12,8,768]{3,2,1,0:T(8,128)(2,1)S(1)} %get-tuple-element.53), channel_id=1, source_target_pairs={{1,0},{2,1},{3,2},{4,3},{5,4},{6,5},{7,6},{8,7},{9,8},{10,9},{11,1... | collective-permute-start | bytes 884744 | tf_op jit(solution)/shard_map/ppermute | solution.py:233
  39.9 6.8 %collective-permute-start.4 = (bf16[2,12,8,768]{3,2,1,0:T(8,128)(2,1)S(1)}, bf16[2,12,8,768]{3,2,1,0:T(8,128)(2,1)S(1)}, u32[]{:S(2)}, u32[]{:S(2)}) collective-permute-start(bf16[2,12,8,768]{3,2,1,0:T(8,128)(2,1)S(1)} %get-tuple-element.54), channel_id=1, source_target_pairs={{0,1},{1,2},{2,3},{3,4},{4,5},{5,6},{6,7},{7,8},{8,9},{9,10},{10,1... | collective-permute-start | bytes 884744 | tf_op jit(solution)/shard_map/ppermute | solution.py:233
  45.5 1.2 copy-start.6
  46.7 0.7 copy-start.7
  59.2 17.7 %collective-permute-start.6 = (bf16[2,20,8,768]{3,2,1,0:T(8,128)(2,1)}, bf16[2,20,8,768]{3,2,1,0:T(8,128)(2,1)S(1)}, u32[]{:S(2)}, u32[]{:S(2)}) collective-permute-start(bf16[2,20,8,768]{3,2,1,0:T(8,128)(2,1)} %get-tuple-element.37), channel_id=1, source_target_pairs={{0,1},{1,2},{2,3},{3,4},{4,5},{5,6},{6,7},{7,8},{8,9},{9,10},{10,1... | collective-permute-start | bytes 1474568 | tf_op jit(solution)/shard_map/ppermute | solution.py:233
  63.6 13.3 %collective-permute-start.7 = (bf16[2,20,8,768]{3,2,1,0:T(8,128)(2,1)}, bf16[2,20,8,768]{3,2,1,0:T(8,128)(2,1)S(1)}, u32[]{:S(2)}, u32[]{:S(2)}) collective-permute-start(bf16[2,20,8,768]{3,2,1,0:T(8,128)(2,1)} %get-tuple-element.38), channel_id=1, source_target_pairs={{1,0},{2,1},{3,2},{4,3},{5,4},{6,5},{7,6},{8,7},{9,8},{10,9},{11,1... | collective-permute-start | bytes 1474568 | tf_op jit(solution)/shard_map/ppermute | solution.py:233
  76.9 0.8 copy-start
  76.9 0.9 copy-start.1
  80.3 52.8 %collective-permute-start.8 = (bf16[2,6,16,768]{3,2,1,0:T(8,128)(2,1)}, bf16[2,6,16,768]{3,2,1,0:T(8,128)(2,1)S(1)}, u32[]{:S(2)}, u32[]{:S(2)}) collective-permute-start(bf16[2,6,16,768]{3,2,1,0:T(8,128)(2,1)} %get-tuple-element.47), channel_id=1, source_target_pairs={{0,32},{32,64},{64,96},{96,128},{128,160},{160,192},{192,224},{224... | collective-permute-start | bytes 884744 | tf_op jit(solution)/shard_map/ppermute | solution.py:233
  82.0 51.1 %collective-permute-start.9 = (bf16[2,6,16,768]{3,2,1,0:T(8,128)(2,1)}, bf16[2,6,16,768]{3,2,1,0:T(8,128)(2,1)S(1)}, u32[]{:S(2)}, u32[]{:S(2)}) collective-permute-start(bf16[2,6,16,768]{3,2,1,0:T(8,128)(2,1)} %get-tuple-element.48), channel_id=1, source_target_pairs={{32,0},{64,32},{96,64},{128,96},{160,128},{192,160},{224,192},{256... | collective-permute-start | bytes 884744 | tf_op jit(solution)/shard_map/ppermute | solution.py:233
  133.1 0.7 copy-start.4
  133.1 0.8 copy-start.5

commit v2 on v1

--- a/solution.py
+++ b/solution.py
@@ -20,6 +20,7 @@
 RAD = 6
 SPAN = 13
 TILE = 128
+PAIRS = 6
 
 
 def dot(a, b, dims, precision=None):
@@ -96,24 +97,27 @@
             out_ref[0, at, :] = value + mask_ref[at, :]
 
 
+def apart(x):
+    first = iota((TILE, TILE), 1) < 64
+    return jnp.concatenate([jnp.where(first, x, 0.0), jnp.where(first, 0.0, x)], 0)
+
+
+def together(x):
+    head_row = iota((TILE, TILE), 0) < 64
+    return jnp.transpose(jnp.where(head_row, x[:, :TILE], x[:, TILE:]))
+
+
 def attend_body(
-    ext_ref, bias_ref, q_ref, g_ref, k_ref, v_ref, t_ref, b_ref, l_ref, r_ref, lc_ref, rc_ref,
+    ext_ref, bias_ref, q_ref, g_ref, k_ref, v_ref, t_ref, b_ref, l_ref, r_ref,
     out_ref, dq_ref, own_ref, top_ref, bottom_ref, left_ref, right_ref, part_ref,
     kw_ref, vw_ref, sum_ref,
 ):
-    pair = pl.program_id(0)
     for n, (own, window) in enumerate(((k_ref, kw_ref), (v_ref, vw_ref))):
         window[0:6, 0:16] = t_ref[n]
         window[6:14, 0:16] = own[...]
         window[14:20, 0:16] = b_ref[n]
-        window[0:6, 16:24] = lc_ref[n, 0:6]
-        window[6:14, 16:24] = l_ref[n]
-        window[14:20, 16:24] = lc_ref[n, 6:12]
-        window[0:6, 24:32] = rc_ref[n, 0:6]
-        window[6:14, 24:32] = r_ref[n]
-        window[14:20, 24:32] = rc_ref[n, 6:12]
-    keys = kw_ref[...].reshape(ROWS * SLOTS, TILE)
-    values = vw_ref[...].reshape(ROWS * SLOTS, TILE)
+        window[:, 16:24] = l_ref[n]
+        window[:, 24:32] = r_ref[n]
 
     row, col = lax.axis_index("row"), lax.axis_index("col")
     panel = row // 2
@@ -121,87 +125,86 @@
     valid = ((row % 2) * 8 + (token >> 4) < ext_ref[0, panel, col]) & (
         (token & 15) < ext_ref[1, panel, col]
     )
-    first = iota((TILE, TILE), 1) < 64
-    queries = q_ref[...].reshape(TILE, TILE).astype(jnp.float32) * 0.125
-    grads = jnp.where(valid, g_ref[...].reshape(TILE, TILE).astype(jnp.float32), 0.0)
-
-    def apart(x):
-        return jnp.concatenate([jnp.where(first, x, 0.0), jnp.where(first, 0.0, x)], 0)
-
-    grads_f = apart(grads)
-    queries_b = apart(queries).astype(jnp.bfloat16)
-    grads_b = grads_f.astype(jnp.bfloat16)
-
-    score = dot(keys, queries_b, NT)
-    score = score + jnp.concatenate([bias_ref[0], bias_ref[1]], 1)
-    highest = jnp.max(score, axis=0, keepdims=True)
-    weights = jnp.exp(score - highest)
-    prob = weights * (1.0 / jnp.sum(weights, axis=0, keepdims=True))
-    prob_b = prob.astype(jnp.bfloat16)
-    output = dot(values, prob_b, TN)
-    delta = jnp.sum(jnp.transpose(grads_f) * output, axis=0, keepdims=True)
-    dprob = dot(values, grads_b, NT)
-    dscore = prob * (dprob - delta)
-    dscore_b = dscore.astype(jnp.bfloat16)
-
-    head_row = iota((TILE, TILE), 0) < 64
-
-    def together(x):
-        return jnp.transpose(jnp.where(head_row, x[:, :TILE], x[:, TILE:]))
-
-    attended = jnp.where(valid, together(output), 0.0)
-    out_ref[...] = attended.astype(jnp.bfloat16).reshape(8, 16, TILE)
-    dq = together(dot(keys, dscore_b, TN)) * 0.125
-    dq_ref[...] = dq.astype(jnp.bfloat16).reshape(8, 16, TILE)
-    dk = dot(dscore_b, queries_b, NN)
-    dv = dot(prob_b, grads_b, NN)
-    for n, grad in enumerate((dk, dv)):
-        grad = grad.reshape(ROWS, SLOTS, TILE)
-        top_ref[n] = grad[0:6, 0:16]
-        own_ref[n] = grad[6:14, 0:16]
-        bottom_ref[n] = grad[14:20, 0:16]
-        left_ref[n] = grad[:, 16:24].astype(jnp.bfloat16)
-        right_ref[n] = grad[:, 24:32].astype(jnp.bfloat16)
-
-    @pl.when(pair == 0)
-    def _():
-        sum_ref[...] = jnp.zeros_like(sum_ref)
+    pairs = range(PAIRS)
+    at = [slice(p * TILE, (p + 1) * TILE) for p in pairs]
+    keys = [kw_ref[:, :, a].reshape(ROWS * SLOTS, TILE) for a in at]
+    values = [vw_ref[:, :, a].reshape(ROWS * SLOTS, TILE) for a in at]
+    queries_b = [
+        apart(q_ref[:, :, a].reshape(TILE, TILE).astype(jnp.float32) * 0.125).astype(jnp.bfloat16)
+        for a in at
+    ]
+    grads_f = [
+        apart(jnp.where(valid, g_ref[:, :, a].reshape(TILE, TILE).astype(jnp.float32), 0.0)) for a in at
+    ]
+    grads_b = [x.astype(jnp.bfloat16) for x in grads_f]
+
+    prob, prob_b = [], []
+    for p in pairs:
+        score = dot(keys[p], queries_b[p], NT)
+        score = score + jnp.concatenate([bias_ref[2 * p], bias_ref[2 * p + 1]], 1)
+        highest = jnp.max(score, axis=0, keepdims=True)
+        weights = jnp.exp(score - highest)
+        prob.append(weights * (1.0 / jnp.sum(weights, axis=0, keepdims=True)))
+        prob_b.append(prob[p].astype(jnp.bfloat16))
+    dscore, dscore_b = [], []
+    for p in pairs:
+        output = dot(values[p], prob_b[p], TN)
+        delta = jnp.sum(jnp.transpose(grads_f[p]) * output, axis=0, keepdims=True)
+        attended = jnp.where(valid, together(output), 0.0)
+        out_ref[:, :, at[p]] = attended.astype(jnp.bfloat16).reshape(8, 16, TILE)
+        dprob = dot(values[p], grads_b[p], NT)
+        dscore.append(prob[p] * (dprob - delta))
+        dscore_b.append(dscore[p].astype(jnp.bfloat16))
+
+    sum_ref[...] = jnp.zeros_like(sum_ref)
 
     offset, query_row = slot_offset()
-    for head in range(2):
-        part = dscore[:, head * TILE : (head + 1) * TILE]
-        low = jnp.zeros((SLOTS, TILE), jnp.float32)
-        high = jnp.zeros((SLOTS, TILE), jnp.float32)
-
-        def line(j, part=part):
-            return part[j * SLOTS : (j + 1) * SLOTS]
-
-        for turn in range(8):
-            x = line(turn)
-            y = line(turn + 8)
-            if turn < 7:
-                x = x + jnp.where(query_row > turn, y, 0.0)
-                y = jnp.where(query_row > turn, 0.0, y)
-            if turn + 16 < ROWS:
-                y = y + line(turn + 16)
-            back = (TILE - 16 * turn) % TILE
-            low = low + (pltpu.roll(x, back, 1) if turn else x)
-            high = high + (pltpu.roll(y, back, 1) if turn else y)
-        for b in range(SPAN):
-            hit = offset == b
-            sum_ref[2 * pair + head, b : b + 1, :TILE] = jnp.sum(
-                jnp.where(hit, low, 0.0), axis=0, keepdims=True
-            )
-            sum_ref[2 * pair + head, b : b + 1, TILE:] = jnp.sum(
-                jnp.where(hit, high, 0.0), axis=0, keepdims=True
-            )
-
-    @pl.when(pair == pl.num_programs(0) - 1)
-    def _():
-        pick = row_pick(0)
-        for half in range(2):
-            sums = sum_ref[half * 8 : half * 8 + 8].reshape(TILE, 2 * TILE)
-            part_ref[half * 16 : half * 16 + 16, :] = dot(pick, sums, NT, HIGH)
+    for p in pairs:
+        dq = together(dot(keys[p], dscore_b[p], TN)) * 0.125
+        dq_ref[:, :, at[p]] = dq.astype(jnp.bfloat16).reshape(8, 16, TILE)
+        dk = dot(dscore_b[p], queries_b[p], NN)
+        dv = dot(prob_b[p], grads_b[p], NN)
+        for n, grad in enumerate((dk, dv)):
+            grad = grad.reshape(ROWS, SLOTS, TILE)
+            top_ref[n, :, :, at[p]] = grad[0:6, 0:16]
+            own_ref[n, :, :, at[p]] = grad[6:14, 0:16]
+            bottom_ref[n, :, :, at[p]] = grad[14:20, 0:16]
+            left_ref[n, :, :, at[p]] = grad[:, 16:24].astype(jnp.bfloat16)
+            right_ref[n, :, :, at[p]] = grad[:, 24:32].astype(jnp.bfloat16)
+
+        for head in range(2):
+            part = dscore[p][:, head * TILE : (head + 1) * TILE]
+            low = jnp.zeros((SLOTS, TILE), jnp.float32)
+            high = jnp.zeros((SLOTS, TILE), jnp.float32)
+
+            def line(j, part=part):
+                return part[j * SLOTS : (j + 1) * SLOTS]
+
+            for turn in range(8):
+                x = line(turn)
+                y = line(turn + 8)
+                if turn < 7:
+                    x = x + jnp.where(query_row > turn, y, 0.0)
+                    y = jnp.where(query_row > turn, 0.0, y)
+                if turn + 16 < ROWS:
+                    y = y + line(turn + 16)
+                back = (TILE - 16 * turn) % TILE
+                low = low + (pltpu.roll(x, back, 1) if turn else x)
+                high = high + (pltpu.roll(y, back, 1) if turn else y)
+            index = 2 * p + head
+            for b in range(SPAN):
+                hit = offset == b
+                sum_ref[index, b : b + 1, :TILE] = jnp.sum(
+                    jnp.where(hit, low, 0.0), axis=0, keepdims=True
+                )
+                sum_ref[index, b : b + 1, TILE:] = jnp.sum(
+                    jnp.where(hit, high, 0.0), axis=0, keepdims=True
+                )
+
+    pick = row_pick(0)
+    for half in range(2):
+        sums = sum_ref[half * 8 : half * 8 + 8].reshape(TILE, 2 * TILE)
+        part_ref[half * 16 : half * 16 + 16, :] = dot(pick, sums, NT, HIGH)
 
 
 def border_body(top_ref, bottom_ref, fl_ref, fr_ref, up_ref, down_ref):
@@ -245,6 +248,7 @@
     return jax.ShapeDtypeStruct(dims, dtype)
 
 
+LIMIT = 32 << 20
 SMEM = pl.BlockSpec(memory_space=pltpu.SMEM)
 VMEM = pl.BlockSpec(memory_space=pltpu.VMEM)
 
@@ -255,8 +259,6 @@
     both = jnp.stack([keys, values])
     top = neighbour(both[:, 2:], "row", 1)
     bottom = neighbour(both[:, :6], "row", -1)
-    left = neighbour(both[:, :, EDGE:], "col", 1)
-    right = neighbour(both[:, :, :EDGE], "col", -1)
 
     table = jnp.pad(jnp.swapaxes(rel_bias, 1, 2), ((0, 0), (0, 3), (0, 3)))
     bias = pl.pallas_call(
@@ -267,23 +269,17 @@
         out_specs=pl.BlockSpec((1, ROWS * SLOTS, TILE), lambda h: (h, 0, 0)),
         scratch_shapes=[pltpu.VMEM((ROWS * SLOTS, TILE), jnp.float32)],
         cost_estimate=pl.CostEstimate(flops=20_000_000, bytes_accessed=4_000_000, transcendentals=0),
+        compiler_params=pltpu.CompilerParams(vmem_limit_bytes=LIMIT),
         name="bias_mask",
     )(extents, table)
 
-    top, bottom, left, right, bias = lax.optimization_barrier((top, bottom, left, right, bias))
-    ends = jnp.concatenate([top, bottom], 1)
-    left_ends = neighbour(ends[:, :, EDGE:], "col", 1)
-    right_ends = neighbour(ends[:, :, :EDGE], "col", -1)
-
-    def lanes(*dims):
-        return pl.BlockSpec(dims + (TILE,), lambda g: (0,) * len(dims) + (g,))
-
-    tile = lanes(8, 16)
-    rows_spec, edge_spec, ends_spec = lanes(2, 6, 16), lanes(2, 8, EDGE), lanes(2, 12, EDGE)
-    side_spec = lanes(2, ROWS, EDGE)
+    top, bottom, bias = lax.optimization_barrier((top, bottom, bias))
+    band = jnp.concatenate([top, both, bottom], 1)
+    left = neighbour(band[:, :, EDGE:], "col", 1)
+    right = neighbour(band[:, :, :EDGE], "col", -1)
+
     attended, d_queries, own, d_top, d_bottom, d_left, d_right, part = pl.pallas_call(
         attend_body,
-        grid=(width // TILE,),
         out_shape=(
             shape(queries.shape),
             shape(queries.shape),
@@ -294,40 +290,36 @@
             shape((2, ROWS, EDGE, width)),
             shape((32, TILE), jnp.float32),
         ),
-        in_specs=[
-            SMEM,
-            pl.BlockSpec((2, ROWS * SLOTS, TILE), lambda g: (g, 0, 0)),
-            tile, tile, tile, tile,
-            rows_spec, rows_spec, edge_spec, edge_spec, ends_spec, ends_spec,
-        ],
-        out_specs=(
-            tile, tile, lanes(2, 8, 16), rows_spec, rows_spec, side_spec, side_spec,
-            pl.BlockSpec((32, TILE), lambda g: (0, 0)),
-        ),
+        in_specs=[SMEM] + [VMEM] * 9,
+        out_specs=(VMEM,) * 8,
         scratch_shapes=[
-            pltpu.VMEM((ROWS, SLOTS, TILE), jnp.bfloat16),
-            pltpu.VMEM((ROWS, SLOTS, TILE), jnp.bfloat16),
+            pltpu.VMEM((ROWS, SLOTS, PAIRS * TILE), jnp.bfloat16),
+            pltpu.VMEM((ROWS, SLOTS, PAIRS * TILE), jnp.bfloat16),
             pltpu.VMEM((16, 16, 2 * TILE), jnp.float32),
         ],
         cost_estimate=pl.CostEstimate(
             flops=1_500_000_000, bytes_accessed=9_000_000, transcendentals=1_000_000
         ),
+        compiler_params=pltpu.CompilerParams(vmem_limit_bytes=LIMIT),
         name="attend",
-    )(extents, bias, queries, d_out, keys, values, top, bottom, left, right, left_ends, right_ends)
-
+    )(extents, bias, queries, d_out, keys, values, top, bottom, left, right)
+
+    piece = exchange(part.reshape(lax.axis_size("col"), -1, TILE), "col")
+    d_left, d_right, piece = lax.optimization_barrier((d_left, d_right, piece))
     from_left = neighbour(d_right, "col", 1)
     from_right = neighbour(d_left, "col", -1)
-    piece = exchange(part.reshape(lax.axis_size("col"), -1, TILE), "col")
+    piece = gathered(jnp.sum(piece, 0), "row")
     from_left, from_right, piece = lax.optimization_barrier((from_left, from_right, piece))
     up, down = pl.pallas_call(
         border_body,
         out_shape=(shape(d_top.shape), shape(d_top.shape)),
         in_specs=[VMEM] * 4,
         out_specs=(VMEM, VMEM),
+        compiler_params=pltpu.CompilerParams(vmem_limit_bytes=LIMIT),
         name="border",
     )(d_top, d_bottom, from_left, from_right)
     up, down, piece = lax.optimization_barrier((up, down, piece))
-    total = gathered(jnp.sum(gathered(jnp.sum(piece, 0), "row"), 0), "col").reshape(part.shape)
+    total = gathered(jnp.sum(piece, 0), "col").reshape(part.shape)
     from_below = neighbour(up, "row", -1)
     from_above = neighbour(down, "row", 1)
     d_keys, d_values, d_rel_bias = pl.pallas_call(
@@ -335,6 +327,7 @@
         out_shape=(shape(keys.shape), shape(keys.shape), shape(rel_bias.shape, jnp.float32)),
         in_specs=[VMEM] * 6,
         out_specs=(VMEM, VMEM, VMEM),
+        compiler_params=pltpu.CompilerParams(vmem_limit_bytes=LIMIT),
         name="final",
     )(own, from_left, from_right, from_above, from_below, total)
     return (attended, d_queries, d_keys, d_values, d_rel_bias)

time: 138 us -> 117 us (0.85)
  the two profiles are of different devices: /device:TPU:1 before, /device:TPU:4 now
where the time goes in v2:
time: 117 us; the launch traced here: 116 us
  blocking collectives  52.5 us (45%)
  starting transfers between devices  36.8 us (31%)
  Pallas kernels  12 us (10%)
  waiting for transfers between devices  10.9 us (9%)
  local copies, waits for them, and re-layouts  1.88 us (2%)
  other arithmetic  1.44 us (1%)
    all_to_all x3, blocking collectives, exchange(): return lax.all_to_all(value, axis, 0, 0)  52.5 us
    ppermute x8, starting transfers between devices, neighbour(): lax.ppermute(value, axis, [(i, i + step) for i in range(size) if 0 <= i +...  36.8 us
    ppermute x8, waiting for transfers between devices, neighbour(): lax.ppermute(value, axis, [(i, i + step) for i in range(size) if 0 <= i +...  10.9 us
    pallas_call x1, Pallas kernels, shards(): pl.pallas_call(attend_body, out_shape=(shape(queries.shape), shape(querie...  6.06 us
    pallas_call x1, Pallas kernels, shards(): pl.pallas_call(bias_body, grid=(heads,), out_shape=shape((heads, ROWS * S...  5.01 us
  transfers between devices with their start and end apart: 8, of which 2 were waited for; matrix products, arithmetic and copies ran while one was open for 1% of the time, Pallas kernels for 4%

profile of v2, /device:TPU:4, one launch (start us, length us, event | category | flops | bytes accessed | tf_op | source)
XLA Modules:
  0.0 116.3 jit_solution(11109017961028809373)
XLA Ops:
  0.6 0.0 copy-start.1
  0.6 0.0 copy-start
  0.7 1.2 %pad_maximum_fusion.1 = (bf16[2,6,16,768]{3,2,1,0:T(8,128)(2,1)S(1)}, bf16[2,6,16,768]{3,2,1,0:T(8,128)(2,1)S(1)}) fusion(bf16[1,8,16,768]{3,2,1,0:T(8,128)(2,1)} %bitcast.9, bf16[1,8,16,768]{3,2,1,0:T(8,128)(2,1)} %bitcast.7), kind=kLoop, calls=%fused_computation.4 | loop fusion | flops 294912 | bytes 983040 | tf_op jit(solution)/shard_map/stack | solution.py:259
  1.9 18.2 %collective-permute-start.1 = (bf16[2,6,16,768]{3,2,1,0:T(8,128)(2,1)S(1)}, bf16[2,6,16,768]{3,2,1,0:T(8,128)(2,1)S(1)}, u32[]{:S(2)}, u32[]{:S(2)}) collective-permute-start(bf16[2,6,16,768]{3,2,1,0:T(8,128)(2,1)S(1)} %get-tuple-element.57), channel_id=1, source_target_pairs={{32,0},{64,32},{96,64},{128,96},{160,128},{192,160},{224,192},{256... | collective-permute-start | bytes 884744 | tf_op jit(solution)/shard_map/ppermute | solution.py:236
  20.1 1.9 %collective-permute-start = (bf16[2,6,16,768]{3,2,1,0:T(8,128)(2,1)S(1)}, bf16[2,6,16,768]{3,2,1,0:T(8,128)(2,1)S(1)}, u32[]{:S(2)}, u32[]{:S(2)}) collective-permute-start(bf16[2,6,16,768]{3,2,1,0:T(8,128)(2,1)S(1)} %get-tuple-element.58), channel_id=1, source_target_pairs={{0,32},{32,64},{64,96},{96,128},{128,160},{160,192},{192,224},{224... | collective-permute-start | bytes 884744 | tf_op jit(solution)/shard_map/ppermute | solution.py:236
  22.0 1.0 copy.12
  23.0 0.0 copy-start.4
  23.1 0.7 copy-done.4
  23.8 0.0 copy-start.2
  23.8 0.0 copy-start.3
  23.8 5.0 %bias_mask.1.bias_ref = f32[12,640,128]{2,1,0:T(8,128)S(1)} custom-call(s32[2,16,32]{2,1,0:T(8,128)S(1)} %copy-done.4, f32[12,16,16]{2,1,0:T(8,128)S(1)} %pad.4.table_ref), custom_call_target="tpu_custom_call" | custom-call | flops 20000000 | bytes 4000000 | tf_op jit(solution)/shard_map/bias_mask/pallas_call | solution.py:264
  28.8 0.0 collective-permute-done.1.b_ref
  28.8 9.4 %collective-permute-done.t_ref = bf16[2,6,16,768]{3,2,1,0:T(8,128)(2,1)S(1)} collective-permute-done((bf16[2,6,16,768]{3,2,1,0:T(8,128)(2,1)S(1)}, bf16[2,6,16,768]{3,2,1,0:T(8,128)(2,1)S(1)}, u32[]{:S(2)}, u32[]{:S(2)}) %collective-permute-start) | collective-permute-done | bytes 294944 | tf_op jit(solution)/shard_map/ppermute | solution.py:236
  38.2 0.0 copy-done.1
  38.2 0.0 copy-done
  38.2 0.1 pad_maximum_fusion
  38.4 0.1 fusion.1
  38.4 1.3 %collective-permute-start.3 = (bf16[2,20,8,768]{3,2,1,0:T(8,128)(2,1)S(1)}, bf16[2,20,8,768]{3,2,1,0:T(8,128)(2,1)S(1)}, u32[]{:S(2)}, u32[]{:S(2)}) collective-permute-start(bf16[2,20,8,768]{3,2,1,0:T(8,128)(2,1)S(1)} %get-tuple-element.55), channel_id=1, source_target_pairs={{1,0},{2,1},{3,2},{4,3},{5,4},{6,5},{7,6},{8,7},{9,8},{10,9},{11,1... | collective-permute-start | bytes 1474568 | tf_op jit(solution)/shard_map/ppermute | solution.py:236
  39.7 3.1 %collective-permute-start.2 = (bf16[2,20,8,768]{3,2,1,0:T(8,128)(2,1)S(1)}, bf16[2,20,8,768]{3,2,1,0:T(8,128)(2,1)S(1)}, u32[]{:S(2)}, u32[]{:S(2)}) collective-permute-start(bf16[2,20,8,768]{3,2,1,0:T(8,128)(2,1)S(1)} %get-tuple-element.56), channel_id=1, source_target_pairs={{0,1},{1,2},{2,3},{3,4},{4,5},{5,6},{6,7},{7,8},{8,9},{9,10},{10,1... | collective-permute-start | bytes 1474568 | tf_op jit(solution)/shard_map/ppermute | solution.py:236
  42.8 0.0 collective-permute-done.3.r_ref
  42.8 1.4 %collective-permute-done.2.l_ref = bf16[2,20,8,768]{3,2,1,0:T(8,128)(2,1)S(1)} collective-permute-done((bf16[2,20,8,768]{3,2,1,0:T(8,128)(2,1)S(1)}, bf16[2,20,8,768]{3,2,1,0:T(8,128)(2,1)S(1)}, u32[]{:S(2)}, u32[]{:S(2)}) %collective-permute-start.2) | collective-permute-done | bytes 491552 | tf_op jit(solution)/shard_map/ppermute | solution.py:236
  44.2 0.0 copy-done.2
  44.2 0.0 copy-done.3
  44.2 6.1 %attend.1 = (bf16[8,16,768]{2,1,0:T(8,128)(2,1)}, bf16[8,16,768]{2,1,0:T(8,128)(2,1)}, f32[2,8,16,768]{3,2,1,0:T(8,128)S(1)}, f32[2,6,16,768]{3,2,1,0:T(8,128)S(...) custom-call(s32[2,16,32]{2,1,0:T(8,128)S(1)} %copy-done.4, ...), custom_call_target="tpu_custom_call" | custom-call | flops 1500000000 | bytes 9000000 | tf_op jit(solution)/shard_map/attend/pallas_call | solution.py:281
  50.3 20.5 %all_to_all.15 = f32[32,1,128]{2,1,0:T(1,128)S(1)} all-to-all(f32[32,1,128]{2,1,0:T(1,128)S(1)} %bitcast.12), channel_id=1, replica_groups=mesh['row'=32,'col'=32] {'col'}, dimensions={0} | all-to-all | bytes 32768 | tf_op jit(solution)/shard_map/all_to_all | solution.py:240
  70.8 1.6 %collective-permute-start.4 = (bf16[2,20,8,768]{3,2,1,0:T(8,128)(2,1)}, bf16[2,20,8,768]{3,2,1,0:T(8,128)(2,1)S(1)}, u32[]{:S(2)}, u32[]{:S(2)}) collective-permute-start(bf16[2,20,8,768]{3,2,1,0:T(8,128)(2,1)} %get-tuple-element.39), channel_id=1, source_target_pairs={{0,1},{1,2},{2,3},{3,4},{4,5},{5,6},{6,7},{7,8},{8,9},{9,10},{10,1... | collective-permute-start | bytes 1474568 | tf_op jit(solution)/shard_map/ppermute | solution.py:236
  72.4 1.3 %collective-permute-start.5 = (bf16[2,20,8,768]{3,2,1,0:T(8,128)(2,1)S(1)}, bf16[2,20,8,768]{3,2,1,0:T(8,128)(2,1)S(1)}, u32[]{:S(2)}, u32[]{:S(2)}) collective-permute-start(bf16[2,20,8,768]{3,2,1,0:T(8,128)(2,1)S(1)} %get-tuple-element.40), channel_id=1, source_target_pairs={{1,0},{2,1},{3,2},{4,3},{5,4},{6,5},{7,6},{8,7},{9,8},{10,9},{11,1... | collective-permute-start | bytes 1474568 | tf_op jit(solution)/shard_map/ppermute | solution.py:236
  73.7 0.1 reduce_sum.18
  73.8 16.9 %all_to_all.16 = f32[32,1,128]{2,1,0:T(1,128)S(1)} all-to-all(f32[32,1,128]{2,1,0:T(1,128)S(1)} %broadcast_in_dim.6), channel_id=1, replica_groups=mesh['row'=32,'col'=32] {'row'}, dimensions={0} | all-to-all | bytes 32768 | tf_op jit(solution)/shard_map/all_to_all | solution.py:240
  90.7 0.0 collective-permute-done.4.fl_ref
  90.7 0.0 collective-permute-done.5.fr_ref
  90.7 0.1 border.1
  90.8 2.3 %collective-permute-start.6 = (bf16[2,6,16,768]{3,2,1,0:T(8,128)(2,1)S(1)}, bf16[2,6,16,768]{3,2,1,0:T(8,128)(2,1)S(1)}, u32[]{:S(2)}, u32[]{:S(2)}) collective-permute-start(bf16[2,6,16,768]{3,2,1,0:T(8,128)(2,1)S(1)} %get-tuple-element.49), channel_id=1, source_target_pairs={{0,32},{32,64},{64,96},{96,128},{128,160},{160,192},{192,224},{224... | collective-permute-start | bytes 884744 | tf_op jit(solution)/shard_map/ppermute | solution.py:236
  93.1 7.1 %collective-permute-start.7 = (bf16[2,6,16,768]{3,2,1,0:T(8,128)(2,1)S(1)}, bf16[2,6,16,768]{3,2,1,0:T(8,128)(2,1)S(1)}, u32[]{:S(2)}, u32[]{:S(2)}) collective-permute-start(bf16[2,6,16,768]{3,2,1,0:T(8,128)(2,1)S(1)} %get-tuple-element.50), channel_id=1, source_target_pairs={{32,0},{64,32},{96,64},{128,96},{160,128},{192,160},{224,192},{256... | collective-permute-start | bytes 884744 | tf_op jit(solution)/shard_map/ppermute | solution.py:236
  100.3 0.1 reduce_sum.19
  100.3 15.1 %all_to_all.17 = f32[32,1,128]{2,1,0:T(1,128)S(1)} all-to-all(f32[32,1,128]{2,1,0:T(1,128)S(1)} %broadcast_in_dim.7), channel_id=1, replica_groups=mesh['row'=32,'col'=32] {'col'}, dimensions={0} | all-to-all | bytes 32768 | tf_op jit(solution)/shard_map/all_to_all | solution.py:240
  115.5 0.0 collective-permute-done.6.fu_ref
  115.5 0.0 collective-permute-done.7.fd_ref
  115.5 0.9 final.1
  (3 shorter events, 0.0 us)
Async XLA Ops:
  0.6 37.6 %copy-start.1 = (bf16[8,16,768]{2,1,0:T(8,128)(2,1)S(1)}, bf16[8,16,768]{2,1,0:T(8,128)(2,1)}, u32[]{:S(2)}) copy-start(bf16[8,16,768]{2,1,0:T(8,128)(2,1)} %v_ref.1) | copy-start | bytes 589828
  0.6 37.6 %copy-start = (bf16[8,16,768]{2,1,0:T(8,128)(2,1)S(1)}, bf16[8,16,768]{2,1,0:T(8,128)(2,1)}, u32[]{:S(2)}) copy-start(bf16[8,16,768]{2,1,0:T(8,128)(2,1)} %k_ref.1) | copy-start | bytes 589828
  1.9 26.9 %collective-permute-start.1 = (bf16[2,6,16,768]{3,2,1,0:T(8,128)(2,1)S(1)}, bf16[2,6,16,768]{3,2,1,0:T(8,128)(2,1)S(1)}, u32[]{:S(2)}, u32[]{:S(2)}) collective-permute-start(bf16[2,6,16,768]{3,2,1,0:T(8,128)(2,1)S(1)} %get-tuple-element.57), channel_id=1, source_target_pairs={{32,0},{64,32},{96,64},{128,96},{160,128},{192,160},{224,192},{256... | collective-permute-start | bytes 884744 | tf_op jit(solution)/shard_map/ppermute | solution.py:236
  20.1 18.2 %collective-permute-start = (bf16[2,6,16,768]{3,2,1,0:T(8,128)(2,1)S(1)}, bf16[2,6,16,768]{3,2,1,0:T(8,128)(2,1)S(1)}, u32[]{:S(2)}, u32[]{:S(2)}) collective-permute-start(bf16[2,6,16,768]{3,2,1,0:T(8,128)(2,1)S(1)} %get-tuple-element.58), channel_id=1, source_target_pairs={{0,32},{32,64},{64,96},{96,128},{128,160},{160,192},{192,224},{224... | collective-permute-start | bytes 884744 | tf_op jit(solution)/shard_map/ppermute | solution.py:236
  23.0 0.7 copy-start.4
  23.8 20.5 %copy-start.2 = (bf16[8,16,768]{2,1,0:T(8,128)(2,1)S(1)}, bf16[8,16,768]{2,1,0:T(8,128)(2,1)}, u32[]{:S(2)}) copy-start(bf16[8,16,768]{2,1,0:T(8,128)(2,1)} %q_ref.1) | copy-start | bytes 589828
  23.8 20.5 %copy-start.3 = (bf16[8,16,768]{2,1,0:T(8,128)(2,1)S(1)}, bf16[8,16,768]{2,1,0:T(8,128)(2,1)}, u32[]{:S(2)}) copy-start(bf16[8,16,768]{2,1,0:T(8,128)(2,1)} %g_ref.1) | copy-start | bytes 589828
  38.4 4.4 %collective-permute-start.3 = (bf16[2,20,8,768]{3,2,1,0:T(8,128)(2,1)S(1)}, bf16[2,20,8,768]{3,2,1,0:T(8,128)(2,1)S(1)}, u32[]{:S(2)}, u32[]{:S(2)}) collective-permute-start(bf16[2,20,8,768]{3,2,1,0:T(8,128)(2,1)S(1)} %get-tuple-element.55), channel_id=1, source_target_pairs={{1,0},{2,1},{3,2},{4,3},{5,4},{6,5},{7,6},{8,7},{9,8},{10,9},{11,1... | collective-permute-start | bytes 1474568 | tf_op jit(solution)/shard_map/ppermute | solution.py:236
  39.7 4.5 %collective-permute-start.2 = (bf16[2,20,8,768]{3,2,1,0:T(8,128)(2,1)S(1)}, bf16[2,20,8,768]{3,2,1,0:T(8,128)(2,1)S(1)}, u32[]{:S(2)}, u32[]{:S(2)}) collective-permute-start(bf16[2,20,8,768]{3,2,1,0:T(8,128)(2,1)S(1)} %get-tuple-element.56), channel_id=1, source_target_pairs={{0,1},{1,2},{2,3},{3,4},{4,5},{5,6},{6,7},{7,8},{8,9},{9,10},{10,1... | collective-permute-start | bytes 1474568 | tf_op jit(solution)/shard_map/ppermute | solution.py:236
  70.8 19.9 %collective-permute-start.4 = (bf16[2,20,8,768]{3,2,1,0:T(8,128)(2,1)}, bf16[2,20,8,768]{3,2,1,0:T(8,128)(2,1)S(1)}, u32[]{:S(2)}, u32[]{:S(2)}) collective-permute-start(bf16[2,20,8,768]{3,2,1,0:T(8,128)(2,1)} %get-tuple-element.39), channel_id=1, source_target_pairs={{0,1},{1,2},{2,3},{3,4},{4,5},{5,6},{6,7},{7,8},{8,9},{9,10},{10,1... | collective-permute-start | bytes 1474568 | tf_op jit(solution)/shard_map/ppermute | solution.py:236
  72.4 18.2 %collective-permute-start.5 = (bf16[2,20,8,768]{3,2,1,0:T(8,128)(2,1)S(1)}, bf16[2,20,8,768]{3,2,1,0:T(8,128)(2,1)S(1)}, u32[]{:S(2)}, u32[]{:S(2)}) collective-permute-start(bf16[2,20,8,768]{3,2,1,0:T(8,128)(2,1)S(1)} %get-tuple-element.40), channel_id=1, source_target_pairs={{1,0},{2,1},{3,2},{4,3},{5,4},{6,5},{7,6},{8,7},{9,8},{10,9},{11,1... | collective-permute-start | bytes 1474568 | tf_op jit(solution)/shard_map/ppermute | solution.py:236
  90.8 24.7 %collective-permute-start.6 = (bf16[2,6,16,768]{3,2,1,0:T(8,128)(2,1)S(1)}, bf16[2,6,16,768]{3,2,1,0:T(8,128)(2,1)S(1)}, u32[]{:S(2)}, u32[]{:S(2)}) collective-permute-start(bf16[2,6,16,768]{3,2,1,0:T(8,128)(2,1)S(1)} %get-tuple-element.49), channel_id=1, source_target_pairs={{0,32},{32,64},{64,96},{96,128},{128,160},{160,192},{192,224},{224... | collective-permute-start | bytes 884744 | tf_op jit(solution)/shard_map/ppermute | solution.py:236
  93.1 22.3 %collective-permute-start.7 = (bf16[2,6,16,768]{3,2,1,0:T(8,128)(2,1)S(1)}, bf16[2,6,16,768]{3,2,1,0:T(8,128)(2,1)S(1)}, u32[]{:S(2)}, u32[]{:S(2)}) collective-permute-start(bf16[2,6,16,768]{3,2,1,0:T(8,128)(2,1)S(1)} %get-tuple-element.50), channel_id=1, source_target_pairs={{32,0},{64,32},{96,64},{128,96},{160,128},{192,160},{224,192},{256... | collective-permute-start | bytes 884744 | tf_op jit(solution)/shard_map/ppermute | solution.py:236

commit v3 on v2

--- a/solution.py
+++ b/solution.py
@@ -108,7 +108,7 @@
 
 
 def attend_body(
-    ext_ref, bias_ref, q_ref, g_ref, k_ref, v_ref, t_ref, b_ref, l_ref, r_ref,
+    ext_ref, bias_ref, q_ref, g_ref, k_ref, v_ref, t_ref, b_ref, near_ref, far_ref,
     out_ref, dq_ref, own_ref, top_ref, bottom_ref, left_ref, right_ref, part_ref,
     kw_ref, vw_ref, sum_ref,
 ):
@@ -116,10 +116,16 @@
         window[0:6, 0:16] = t_ref[n]
         window[6:14, 0:16] = own[...]
         window[14:20, 0:16] = b_ref[n]
-        window[:, 16:24] = l_ref[n]
-        window[:, 24:32] = r_ref[n]
 
     row, col = lax.axis_index("row"), lax.axis_index("col")
+    for parity, l_ref, r_ref in ((0, far_ref, near_ref), (1, near_ref, far_ref)):
+
+        @pl.when(col % 2 == parity)
+        def _(l_ref=l_ref, r_ref=r_ref):
+            for n, window in enumerate((kw_ref, vw_ref)):
+                window[:, 16:24] = l_ref[n]
+                window[:, 24:32] = r_ref[n]
+
     panel = row // 2
     token = iota((TILE, TILE), 0)
     valid = ((row % 2) * 8 + (token >> 4) < ext_ref[0, panel, col]) & (
@@ -207,20 +213,26 @@
         part_ref[half * 16 : half * 16 + 16, :] = dot(pick, sums, NT, HIGH)
 
 
-def border_body(top_ref, bottom_ref, fl_ref, fr_ref, up_ref, down_ref):
+def sides(near, far):
+    near, far = near.astype(jnp.float32), far.astype(jnp.float32)
+    even = lax.axis_index("col") % 2 == 0
+    return jnp.where(even, far, near), jnp.where(even, near, far)
+
+
+def border_body(top_ref, bottom_ref, near_ref, far_ref, up_ref, down_ref):
     for source, rows, target in ((top_ref, slice(0, 6), up_ref), (bottom_ref, slice(14, 20), down_ref)):
         for n in range(2):
-            low = source[n, :, :EDGE] + fl_ref[n, rows].astype(jnp.float32)
-            high = source[n, :, EDGE:] + fr_ref[n, rows].astype(jnp.float32)
+            left, right = sides(near_ref[n, rows], far_ref[n, rows])
+            low = source[n, :, :EDGE] + left
+            high = source[n, :, EDGE:] + right
             target[n] = jnp.concatenate([low, high], 1).astype(jnp.bfloat16)
 
 
-def final_body(own_ref, fl_ref, fr_ref, fu_ref, fd_ref, part_ref, dk_ref, dv_ref, bias_ref):
+def final_body(own_ref, near_ref, far_ref, fu_ref, fd_ref, part_ref, dk_ref, dv_ref, bias_ref):
     for n, target in enumerate((dk_ref, dv_ref)):
         for r in range(8):
-            left = own_ref[n, r, :EDGE] + fl_ref[n, r + RAD].astype(jnp.float32)
-            right = own_ref[n, r, EDGE:] + fr_ref[n, r + RAD].astype(jnp.float32)
-            total = jnp.concatenate([left, right], 0)
+            left, right = sides(near_ref[n, r + RAD], far_ref[n, r + RAD])
+            total = jnp.concatenate([own_ref[n, r, :EDGE] + left, own_ref[n, r, EDGE:] + right], 0)
             if r < RAD:
                 total = total + fu_ref[n, r].astype(jnp.float32)
             if r >= 8 - RAD:
@@ -234,6 +246,11 @@
 def neighbour(value, axis, step):
     size = lax.axis_size(axis)
     return lax.ppermute(value, axis, [(i, i + step) for i in range(size) if 0 <= i + step < size])
+
+
+def swap(value, axis, first):
+    pairs = [(i, i + 1) for i in range(first, lax.axis_size(axis) - 1, 2)]
+    return lax.ppermute(value, axis, pairs + [(j, i) for i, j in pairs])
 
 
 def exchange(value, axis):
@@ -275,8 +292,10 @@
 
     top, bottom, bias = lax.optimization_barrier((top, bottom, bias))
     band = jnp.concatenate([top, both, bottom], 1)
-    left = neighbour(band[:, :, EDGE:], "col", 1)
-    right = neighbour(band[:, :, :EDGE], "col", -1)
+    even = lax.axis_index("col") % 2 == 0
+    low, high = band[:, :, :EDGE], band[:, :, EDGE:]
+    near = swap(jnp.where(even, high, low), "col", 0)
+    far = swap(jnp.where(even, low, high), "col", 1)
 
     attended, d_queries, own, d_top, d_bottom, d_left, d_right, part = pl.pallas_call(
         attend_body,
@@ -302,14 +321,14 @@
         ),
         compiler_params=pltpu.CompilerParams(vmem_limit_bytes=LIMIT),
         name="attend",
-    )(extents, bias, queries, d_out, keys, values, top, bottom, left, right)
+    )(extents, bias, queries, d_out, keys, values, top, bottom, near, far)
 
     piece = exchange(part.reshape(lax.axis_size("col"), -1, TILE), "col")
     d_left, d_right, piece = lax.optimization_barrier((d_left, d_right, piece))
-    from_left = neighbour(d_right, "col", 1)
-    from_right = neighbour(d_left, "col", -1)
+    from_near = swap(jnp.where(even, d_right, d_left), "col", 0)
+    from_far = swap(jnp.where(even, d_left, d_right), "col", 1)
     piece = gathered(jnp.sum(piece, 0), "row")
-    from_left, from_right, piece = lax.optimization_barrier((from_left, from_right, piece))
+    from_near, from_far, piece = lax.optimization_barrier((from_near, from_far, piece))
     up, down = pl.pallas_call(
         border_body,
         out_shape=(shape(d_top.shape), shape(d_top.shape)),
@@ -317,7 +336,7 @@
         out_specs=(VMEM, VMEM),
         compiler_params=pltpu.CompilerParams(vmem_limit_bytes=LIMIT),
         name="border",
-    )(d_top, d_bottom, from_left, from_right)
+    )(d_top, d_bottom, from_near, from_far)
     up, down, piece = lax.optimization_barrier((up, down, piece))
     total = gathered(jnp.sum(piece, 0), "col").reshape(part.shape)
     from_below = neighbour(up, "row", -1)
@@ -329,7 +348,7 @@
         out_specs=(VMEM, VMEM, VMEM),
         compiler_params=pltpu.CompilerParams(vmem_limit_bytes=LIMIT),
         name="final",
-    )(own, from_left, from_right, from_above, from_below, total)
+    )(own, from_near, from_far, from_above, from_below, total)
     return (attended, d_queries, d_keys, d_values, d_rel_bias)
 
 

time: 117 us -> 115 us (0.983)
  waiting for transfers between devices: 10.9 us -> 6.69 us
  starting transfers between devices: 36.8 us -> 39.6 us
  blocking collectives: 52.5 us -> 50.9 us
    ppermute x0 -> x4, starting transfers between devices: none -> 10 us  [swap(): return lax.ppermute(value, axis, pairs + [(j, i) for i, j in pairs])]
    ppermute x8 -> x4, starting transfers between devices: 36.8 us -> 29.5 us  [neighbour(): lax.ppermute(value, axis, [(i, i + step) for i in range(size) if 0 <= i +...]
    ppermute x8 -> x4, waiting for transfers between devices: 10.9 us -> 5.22 us  [neighbour(): lax.ppermute(value, axis, [(i, i + step) for i in range(size) if 0 <= i +...]
    all_to_all x3, blocking collectives: 52.5 us -> 50.9 us  [exchange(): return lax.all_to_all(value, axis, 0, 0)]
    ppermute x0 -> x4, waiting for transfers between devices: none -> 1.47 us  [swap(): return lax.ppermute(value, axis, pairs + [(j, i) for i, j in pairs])]
where the time goes in v3:
time: 115 us; the launch traced here: 114 us
  blocking collectives  50.9 us (44%)
  starting transfers between devices  39.6 us (34%)
  Pallas kernels  12 us (10%)
  waiting for transfers between devices  6.69 us (6%)
  other arithmetic  2.36 us (2%)
  local copies, waits for them, and re-layouts  1.81 us (2%)
    all_to_all x3, blocking collectives, exchange(): return lax.all_to_all(value, axis, 0, 0)  50.9 us
    ppermute x4, starting transfers between devices, neighbour(): lax.ppermute(value, axis, [(i, i + step) for i in range(size) if 0 <= i +...  29.5 us
    ppermute x4, starting transfers between devices, swap(): return lax.ppermute(value, axis, pairs + [(j, i) for i, j in pairs])  10 us
    pallas_call x1, Pallas kernels, shards(): pl.pallas_call(attend_body, out_shape=(shape(queries.shape), shape(querie...  5.94 us
    ppermute x4, waiting for transfers between devices, neighbour(): lax.ppermute(value, axis, [(i, i + step) for i in range(size) if 0 <= i +...  5.22 us
    pallas_call x1, Pallas kernels, shards(): pl.pallas_call(bias_body, grid=(heads,), out_shape=shape((heads, ROWS * S...  5.01 us
  transfers between devices with their start and end apart: 8, of which 2 were waited for; matrix products, arithmetic and copies ran while one was open for 1% of the time, Pallas kernels for 4%

profile of v3, /device:TPU:4, one launch (start us, length us, event | category | flops | bytes accessed | tf_op | source)
XLA Modules:
  0.0 114.1 jit_solution(3301196432815804026)
XLA Ops:
  0.6 0.0 copy-start.1
  0.6 0.0 copy-start
  0.7 1.2 %pad_maximum_fusion.1 = (bf16[2,6,16,768]{3,2,1,0:T(8,128)(2,1)S(1)}, bf16[2,6,16,768]{3,2,1,0:T(8,128)(2,1)S(1)}) fusion(bf16[1,8,16,768]{3,2,1,0:T(8,128)(2,1)} %bitcast.9, bf16[1,8,16,768]{3,2,1,0:T(8,128)(2,1)} %bitcast.7), kind=kLoop, calls=%fused_computation.8 | loop fusion | flops 294912 | bytes 983040 | tf_op jit(solution)/shard_map/stack | solution.py:276
  1.9 18.2 %collective-permute-start.1 = (bf16[2,6,16,768]{3,2,1,0:T(8,128)(2,1)S(1)}, bf16[2,6,16,768]{3,2,1,0:T(8,128)(2,1)S(1)}, u32[]{:S(2)}, u32[]{:S(2)}) collective-permute-start(bf16[2,6,16,768]{3,2,1,0:T(8,128)(2,1)S(1)} %get-tuple-element.59), channel_id=1, source_target_pairs={{32,0},{64,32},{96,64},{128,96},{160,128},{192,160},{224,192},{256... | collective-permute-start | bytes 884744 | tf_op jit(solution)/shard_map/ppermute | solution.py:248
  20.1 1.9 %collective-permute-start = (bf16[2,6,16,768]{3,2,1,0:T(8,128)(2,1)S(1)}, bf16[2,6,16,768]{3,2,1,0:T(8,128)(2,1)S(1)}, u32[]{:S(2)}, u32[]{:S(2)}) collective-permute-start(bf16[2,6,16,768]{3,2,1,0:T(8,128)(2,1)S(1)} %get-tuple-element.60), channel_id=1, source_target_pairs={{0,32},{32,64},{64,96},{96,128},{128,160},{160,192},{192,224},{224... | collective-permute-start | bytes 884744 | tf_op jit(solution)/shard_map/ppermute | solution.py:248
  22.0 1.0 copy.12
  23.1 0.0 copy-start.4
  23.1 0.7 copy-done.4
  23.8 0.0 copy-start.2
  23.8 0.0 copy-start.3
  23.8 5.0 %bias_mask.1.bias_ref = f32[12,640,128]{2,1,0:T(8,128)S(1)} custom-call(s32[2,16,32]{2,1,0:T(8,128)S(1)} %copy-done.4, f32[12,16,16]{2,1,0:T(8,128)S(1)} %pad.4.table_ref), custom_call_target="tpu_custom_call" | custom-call | flops 20000000 | bytes 4000000 | tf_op jit(solution)/shard_map/bias_mask/pallas_call | solution.py:281
  28.8 0.0 collective-permute-done.1.b_ref
  28.8 5.2 %collective-permute-done.t_ref = bf16[2,6,16,768]{3,2,1,0:T(8,128)(2,1)S(1)} collective-permute-done((bf16[2,6,16,768]{3,2,1,0:T(8,128)(2,1)S(1)}, bf16[2,6,16,768]{3,2,1,0:T(8,128)(2,1)S(1)}, u32[]{:S(2)}, u32[]{:S(2)}) %collective-permute-start) | collective-permute-done | bytes 294944 | tf_op jit(solution)/shard_map/ppermute | solution.py:248
  34.0 0.0 copy-done.1
  34.0 0.0 copy-done
  34.0 0.1 pad_maximum_fusion
  34.2 0.1 broadcast_select_fusion.2
  34.2 0.7 collective-permute-start.3
  34.9 4.8 %collective-permute-start.2 = (bf16[2,20,8,768]{3,2,1,0:T(8,128)(2,1)S(1)}, bf16[2,20,8,768]{3,2,1,0:T(8,128)(2,1)S(1)}, u32[]{:S(2)}, u32[]{:S(2)}) collective-permute-start(bf16[2,20,8,768]{3,2,1,0:T(8,128)(2,1)S(1)} %get-tuple-element.58), channel_id=1, source_target_pairs={{0,1},{2,3},{4,5},{6,7},{8,9},{10,11},{12,13},{14,15},{16,17},{18,... | collective-permute-start | bytes 1474568 | tf_op jit(solution)/shard_map/ppermute | solution.py:253
  39.8 0.0 collective-permute-done.3.far_ref
  39.8 1.5 %collective-permute-done.2.near_ref = bf16[2,20,8,768]{3,2,1,0:T(8,128)(2,1)S(1)} collective-permute-done((bf16[2,20,8,768]{3,2,1,0:T(8,128)(2,1)S(1)}, bf16[2,20,8,768]{3,2,1,0:T(8,128)(2,1)S(1)}, u32[]{:S(2)}, u32[]{:S(2)}) %collective-permute-start.2) | collective-permute-done | bytes 491552 | tf_op jit(solution)/shard_map/ppermute | solution.py:253
  41.2 0.0 copy-done.2
  41.2 0.0 copy-done.3
  41.2 5.9 %attend.1 = (bf16[8,16,768]{2,1,0:T(8,128)(2,1)}, bf16[8,16,768]{2,1,0:T(8,128)(2,1)}, f32[2,8,16,768]{3,2,1,0:T(8,128)S(1)}, f32[2,6,16,768]{3,2,1,0:T(8,128)S(...) custom-call(s32[2,16,32]{2,1,0:T(8,128)S(1)} %copy-done.4, ...), custom_call_target="tpu_custom_call" | custom-call | flops 1500000000 | bytes 9000000 | tf_op jit(solution)/shard_map/attend/pallas_call | solution.py:300
  47.2 21.6 %all_to_all.15 = f32[32,1,128]{2,1,0:T(1,128)S(1)} all-to-all(f32[32,1,128]{2,1,0:T(1,128)S(1)} %bitcast.12), channel_id=1, replica_groups=mesh['row'=32,'col'=32] {'col'}, dimensions={0} | all-to-all | bytes 32768 | tf_op jit(solution)/shard_map/all_to_all | solution.py:257
  68.8 0.8 broadcast_select_fusion
  69.6 0.7 collective-permute-start.5
  70.3 3.8 %collective-permute-start.4 = (bf16[2,20,8,768]{3,2,1,0:T(8,128)(2,1)S(1)}, bf16[2,20,8,768]{3,2,1,0:T(8,128)(2,1)S(1)}, u32[]{:S(2)}, u32[]{:S(2)}) collective-permute-start(bf16[2,20,8,768]{3,2,1,0:T(8,128)(2,1)S(1)} %get-tuple-element.56), channel_id=1, source_target_pairs={{0,1},{2,3},{4,5},{6,7},{8,9},{10,11},{12,13},{14,15},{16,17},{18,... | collective-permute-start | bytes 1474568 | tf_op jit(solution)/shard_map/ppermute | solution.py:253
  74.1 0.1 reduce_sum.18
  74.2 16.9 %all_to_all.16 = f32[32,1,128]{2,1,0:T(1,128)S(1)} all-to-all(f32[32,1,128]{2,1,0:T(1,128)S(1)} %broadcast_in_dim.6), channel_id=1, replica_groups=mesh['row'=32,'col'=32] {'row'}, dimensions={0} | all-to-all | bytes 32768 | tf_op jit(solution)/shard_map/all_to_all | solution.py:257
  91.1 0.0 collective-permute-done.5.far_ref
  91.1 0.0 collective-permute-done.4.near_ref
  91.1 0.1 border.1
  91.2 2.4 %collective-permute-start.6 = (bf16[2,6,16,768]{3,2,1,0:T(8,128)(2,1)S(1)}, bf16[2,6,16,768]{3,2,1,0:T(8,128)(2,1)S(1)}, u32[]{:S(2)}, u32[]{:S(2)}) collective-permute-start(bf16[2,6,16,768]{3,2,1,0:T(8,128)(2,1)S(1)} %get-tuple-element.49), channel_id=1, source_target_pairs={{0,32},{32,64},{64,96},{96,128},{128,160},{160,192},{192,224},{224... | collective-permute-start | bytes 884744 | tf_op jit(solution)/shard_map/ppermute | solution.py:248
  93.7 7.0 %collective-permute-start.7 = (bf16[2,6,16,768]{3,2,1,0:T(8,128)(2,1)S(1)}, bf16[2,6,16,768]{3,2,1,0:T(8,128)(2,1)S(1)}, u32[]{:S(2)}, u32[]{:S(2)}) collective-permute-start(bf16[2,6,16,768]{3,2,1,0:T(8,128)(2,1)S(1)} %get-tuple-element.50), channel_id=1, source_target_pairs={{32,0},{64,32},{96,64},{128,96},{160,128},{192,160},{224,192},{256... | collective-permute-start | bytes 884744 | tf_op jit(solution)/shard_map/ppermute | solution.py:248
  100.7 0.1 reduce_sum.19
  100.8 12.5 %all_to_all.17 = f32[32,1,128]{2,1,0:T(1,128)S(1)} all-to-all(f32[32,1,128]{2,1,0:T(1,128)S(1)} %broadcast_in_dim.7), channel_id=1, replica_groups=mesh['row'=32,'col'=32] {'col'}, dimensions={0} | all-to-all | bytes 32768 | tf_op jit(solution)/shard_map/all_to_all | solution.py:257
  113.2 0.0 collective-permute-done.6.fu_ref
  113.3 0.0 collective-permute-done.7.fd_ref
  113.3 0.9 final.1
  (3 shorter events, 0.0 us)
Async XLA Ops:
  0.6 33.4 %copy-start.1 = (bf16[8,16,768]{2,1,0:T(8,128)(2,1)S(1)}, bf16[8,16,768]{2,1,0:T(8,128)(2,1)}, u32[]{:S(2)}) copy-start(bf16[8,16,768]{2,1,0:T(8,128)(2,1)} %v_ref.1) | copy-start | bytes 589828
  0.6 33.4 %copy-start = (bf16[8,16,768]{2,1,0:T(8,128)(2,1)S(1)}, bf16[8,16,768]{2,1,0:T(8,128)(2,1)}, u32[]{:S(2)}) copy-start(bf16[8,16,768]{2,1,0:T(8,128)(2,1)} %k_ref.1) | copy-start | bytes 589828
  1.9 26.9 %collective-permute-start.1 = (bf16[2,6,16,768]{3,2,1,0:T(8,128)(2,1)S(1)}, bf16[2,6,16,768]{3,2,1,0:T(8,128)(2,1)S(1)}, u32[]{:S(2)}, u32[]{:S(2)}) collective-permute-start(bf16[2,6,16,768]{3,2,1,0:T(8,128)(2,1)S(1)} %get-tuple-element.59), channel_id=1, source_target_pairs={{32,0},{64,32},{96,64},{128,96},{160,128},{192,160},{224,192},{256... | collective-permute-start | bytes 884744 | tf_op jit(solution)/shard_map/ppermute | solution.py:248
  20.1 14.0 %collective-permute-start = (bf16[2,6,16,768]{3,2,1,0:T(8,128)(2,1)S(1)}, bf16[2,6,16,768]{3,2,1,0:T(8,128)(2,1)S(1)}, u32[]{:S(2)}, u32[]{:S(2)}) collective-permute-start(bf16[2,6,16,768]{3,2,1,0:T(8,128)(2,1)S(1)} %get-tuple-element.60), channel_id=1, source_target_pairs={{0,32},{32,64},{64,96},{96,128},{128,160},{160,192},{192,224},{224... | collective-permute-start | bytes 884744 | tf_op jit(solution)/shard_map/ppermute | solution.py:248
  23.1 0.7 copy-start.4
  23.8 17.4 %copy-start.2 = (bf16[8,16,768]{2,1,0:T(8,128)(2,1)S(1)}, bf16[8,16,768]{2,1,0:T(8,128)(2,1)}, u32[]{:S(2)}) copy-start(bf16[8,16,768]{2,1,0:T(8,128)(2,1)} %q_ref.1) | copy-start | bytes 589828
  23.8 17.5 %copy-start.3 = (bf16[8,16,768]{2,1,0:T(8,128)(2,1)S(1)}, bf16[8,16,768]{2,1,0:T(8,128)(2,1)}, u32[]{:S(2)}) copy-start(bf16[8,16,768]{2,1,0:T(8,128)(2,1)} %g_ref.1) | copy-start | bytes 589828
  34.2 5.5 %collective-permute-start.3 = (bf16[2,20,8,768]{3,2,1,0:T(8,128)(2,1)S(1)}, bf16[2,20,8,768]{3,2,1,0:T(8,128)(2,1)S(1)}, u32[]{:S(2)}, u32[]{:S(2)}) collective-permute-start(bf16[2,20,8,768]{3,2,1,0:T(8,128)(2,1)S(1)} %get-tuple-element.57), channel_id=1, source_target_pairs={{1,2},{3,4},{5,6},{7,8},{9,10},{11,12},{13,14},{15,16},{17,18},{19... | collective-permute-start | bytes 1474568 | tf_op jit(solution)/shard_map/ppermute | solution.py:253
  34.9 6.3 %collective-permute-start.2 = (bf16[2,20,8,768]{3,2,1,0:T(8,128)(2,1)S(1)}, bf16[2,20,8,768]{3,2,1,0:T(8,128)(2,1)S(1)}, u32[]{:S(2)}, u32[]{:S(2)}) collective-permute-start(bf16[2,20,8,768]{3,2,1,0:T(8,128)(2,1)S(1)} %get-tuple-element.58), channel_id=1, source_target_pairs={{0,1},{2,3},{4,5},{6,7},{8,9},{10,11},{12,13},{14,15},{16,17},{18,... | collective-permute-start | bytes 1474568 | tf_op jit(solution)/shard_map/ppermute | solution.py:253
  69.6 21.5 %collective-permute-start.5 = (bf16[2,20,8,768]{3,2,1,0:T(8,128)(2,1)}, bf16[2,20,8,768]{3,2,1,0:T(8,128)(2,1)S(1)}, u32[]{:S(2)}, u32[]{:S(2)}) collective-permute-start(bf16[2,20,8,768]{3,2,1,0:T(8,128)(2,1)} %get-tuple-element.55), channel_id=1, source_target_pairs={{1,2},{3,4},{5,6},{7,8},{9,10},{11,12},{13,14},{15,16},{17,18},{19... | collective-permute-start | bytes 1474568 | tf_op jit(solution)/shard_map/ppermute | solution.py:253
  70.3 20.8 %collective-permute-start.4 = (bf16[2,20,8,768]{3,2,1,0:T(8,128)(2,1)S(1)}, bf16[2,20,8,768]{3,2,1,0:T(8,128)(2,1)S(1)}, u32[]{:S(2)}, u32[]{:S(2)}) collective-permute-start(bf16[2,20,8,768]{3,2,1,0:T(8,128)(2,1)S(1)} %get-tuple-element.56), channel_id=1, source_target_pairs={{0,1},{2,3},{4,5},{6,7},{8,9},{10,11},{12,13},{14,15},{16,17},{18,... | collective-permute-start | bytes 1474568 | tf_op jit(solution)/shard_map/ppermute | solution.py:253
  91.2 22.0 %collective-permute-start.6 = (bf16[2,6,16,768]{3,2,1,0:T(8,128)(2,1)S(1)}, bf16[2,6,16,768]{3,2,1,0:T(8,128)(2,1)S(1)}, u32[]{:S(2)}, u32[]{:S(2)}) collective-permute-start(bf16[2,6,16,768]{3,2,1,0:T(8,128)(2,1)S(1)} %get-tuple-element.49), channel_id=1, source_target_pairs={{0,32},{32,64},{64,96},{96,128},{128,160},{160,192},{192,224},{224... | collective-permute-start | bytes 884744 | tf_op jit(solution)/shard_map/ppermute | solution.py:248
  93.7 19.6 %collective-permute-start.7 = (bf16[2,6,16,768]{3,2,1,0:T(8,128)(2,1)S(1)}, bf16[2,6,16,768]{3,2,1,0:T(8,128)(2,1)S(1)}, u32[]{:S(2)}, u32[]{:S(2)}) collective-permute-start(bf16[2,6,16,768]{3,2,1,0:T(8,128)(2,1)S(1)} %get-tuple-element.50), channel_id=1, source_target_pairs={{32,0},{64,32},{96,64},{128,96},{160,128},{192,160},{224,192},{256... | collective-permute-start | bytes 884744 | tf_op jit(solution)/shard_map/ppermute | solution.py:248

commit v4 on v3

--- a/solution.py
+++ b/solution.py
@@ -108,14 +108,12 @@
 
 
 def attend_body(
-    ext_ref, bias_ref, q_ref, g_ref, k_ref, v_ref, t_ref, b_ref, near_ref, far_ref,
+    ext_ref, bias_ref, q_ref, g_ref, k_ref, v_ref, near_row_ref, far_row_ref, near_ref, far_ref,
     out_ref, dq_ref, own_ref, top_ref, bottom_ref, left_ref, right_ref, part_ref,
     kw_ref, vw_ref, sum_ref,
 ):
     for n, (own, window) in enumerate(((k_ref, kw_ref), (v_ref, vw_ref))):
-        window[0:6, 0:16] = t_ref[n]
         window[6:14, 0:16] = own[...]
-        window[14:20, 0:16] = b_ref[n]
 
     row, col = lax.axis_index("row"), lax.axis_index("col")
     for parity, l_ref, r_ref in ((0, far_ref, near_ref), (1, near_ref, far_ref)):
@@ -125,6 +123,14 @@
             for n, window in enumerate((kw_ref, vw_ref)):
                 window[:, 16:24] = l_ref[n]
                 window[:, 24:32] = r_ref[n]
+
+    for parity, t_ref, b_ref in ((0, far_row_ref, near_row_ref), (1, near_row_ref, far_row_ref)):
+
+        @pl.when(row % 2 == parity)
+        def _(t_ref=t_ref, b_ref=b_ref):
+            for n, window in enumerate((kw_ref, vw_ref)):
+                window[0:6, 0:16] = t_ref[n]
+                window[14:20, 0:16] = b_ref[n]
 
     panel = row // 2
     token = iota((TILE, TILE), 0)
@@ -213,41 +219,41 @@
         part_ref[half * 16 : half * 16 + 16, :] = dot(pick, sums, NT, HIGH)
 
 
-def sides(near, far):
+def sides(near, far, axis="col"):
     near, far = near.astype(jnp.float32), far.astype(jnp.float32)
-    even = lax.axis_index("col") % 2 == 0
+    even = lax.axis_index(axis) % 2 == 0
     return jnp.where(even, far, near), jnp.where(even, near, far)
 
 
-def border_body(top_ref, bottom_ref, near_ref, far_ref, up_ref, down_ref):
-    for source, rows, target in ((top_ref, slice(0, 6), up_ref), (bottom_ref, slice(14, 20), down_ref)):
-        for n in range(2):
+def border_body(top_ref, bottom_ref, near_ref, far_ref, near_out_ref, far_out_ref):
+    even = lax.axis_index("row") % 2 == 0
+    for n in range(2):
+        up, down = [], []
+        for source, rows, target in ((top_ref, slice(0, 6), up), (bottom_ref, slice(14, 20), down)):
             left, right = sides(near_ref[n, rows], far_ref[n, rows])
-            low = source[n, :, :EDGE] + left
-            high = source[n, :, EDGE:] + right
-            target[n] = jnp.concatenate([low, high], 1).astype(jnp.bfloat16)
-
-
-def final_body(own_ref, near_ref, far_ref, fu_ref, fd_ref, part_ref, dk_ref, dv_ref, bias_ref):
+            target.append(
+                jnp.concatenate([source[n, :, :EDGE] + left, source[n, :, EDGE:] + right], 1)
+            )
+        near_out_ref[n] = jnp.where(even, down[0], up[0]).astype(jnp.bfloat16)
+        far_out_ref[n] = jnp.where(even, up[0], down[0]).astype(jnp.bfloat16)
+
+
+def final_body(own_ref, near_ref, far_ref, near_row_ref, far_row_ref, part_ref, dk_ref, dv_ref, bias_ref):
     for n, target in enumerate((dk_ref, dv_ref)):
+        above, below = sides(near_row_ref[n], far_row_ref[n], "row")
         for r in range(8):
             left, right = sides(near_ref[n, r + RAD], far_ref[n, r + RAD])
             total = jnp.concatenate([own_ref[n, r, :EDGE] + left, own_ref[n, r, EDGE:] + right], 0)
             if r < RAD:
-                total = total + fu_ref[n, r].astype(jnp.float32)
+                total = total + above[r]
             if r >= 8 - RAD:
-                total = total + fd_ref[n, r - 8 + RAD].astype(jnp.float32)
+                total = total + below[r - 8 + RAD]
             target[r] = total.astype(jnp.bfloat16)
     for h in range(bias_ref.shape[0]):
         at = (h % 8) * 16
         bias_ref[h] = part_ref[(h // 8) * 16 : (h // 8) * 16 + SPAN, at : at + SPAN]
 
 
-def neighbour(value, axis, step):
-    size = lax.axis_size(axis)
-    return lax.ppermute(value, axis, [(i, i + step) for i in range(size) if 0 <= i + step < size])
-
-
 def swap(value, axis, first):
     pairs = [(i, i + 1) for i in range(first, lax.axis_size(axis) - 1, 2)]
     return lax.ppermute(value, axis, pairs + [(j, i) for i, j in pairs])
@@ -274,8 +280,10 @@
     heads = rel_bias.shape[0]
     width = queries.shape[2]
     both = jnp.stack([keys, values])
-    top = neighbour(both[:, 2:], "row", 1)
-    bottom = neighbour(both[:, :6], "row", -1)
+    even_row = lax.axis_index("row") % 2 == 0
+    upper, lower = both[:, :6], both[:, 2:]
+    near_row = swap(jnp.where(even_row, lower, upper), "row", 0)
+    far_row = swap(jnp.where(even_row, upper, lower), "row", 1)
 
     table = jnp.pad(jnp.swapaxes(rel_bias, 1, 2), ((0, 0), (0, 3), (0, 3)))
     bias = pl.pallas_call(
@@ -290,7 +298,8 @@
         name="bias_mask",
     )(extents, table)
 
-    top, bottom, bias = lax.optimization_barrier((top, bottom, bias))
+    near_row, far_row, bias = lax.optimization_barrier((near_row, far_row, bias))
+    top, bottom = jnp.where(even_row, far_row, near_row), jnp.where(even_row, near_row, far_row)
     band = jnp.concatenate([top, both, bottom], 1)
     even = lax.axis_index("col") % 2 == 0
     low, high = band[:, :, :EDGE], band[:, :, EDGE:]
@@ -321,7 +330,7 @@
         ),
         compiler_params=pltpu.CompilerParams(vmem_limit_bytes=LIMIT),
         name="attend",
-    )(extents, bias, queries, d_out, keys, values, top, bottom, near, far)
+    )(extents, bias, queries, d_out, keys, values, near_row, far_row, near, far)
 
     piece = exchange(part.reshape(lax.axis_size("col"), -1, TILE), "col")
     d_left, d_right, piece = lax.optimization_barrier((d_left, d_right, piece))
@@ -329,7 +338,7 @@
     from_far = swap(jnp.where(even, d_left, d_right), "col", 1)
     piece = gathered(jnp.sum(piece, 0), "row")
     from_near, from_far, piece = lax.optimization_barrier((from_near, from_far, piece))
-    up, down = pl.pallas_call(
+    to_near, to_far = pl.pallas_call(
         border_body,
         out_shape=(shape(d_top.shape), shape(d_top.shape)),
         in_specs=[VMEM] * 4,
@@ -337,10 +346,10 @@
         compiler_params=pltpu.CompilerParams(vmem_limit_bytes=LIMIT),
         name="border",
     )(d_top, d_bottom, from_near, from_far)
-    up, down, piece = lax.optimization_barrier((up, down, piece))
+    to_near, to_far, piece = lax.optimization_barrier((to_near, to_far, piece))
     total = gathered(jnp.sum(piece, 0), "col").reshape(part.shape)
-    from_below = neighbour(up, "row", -1)
-    from_above = neighbour(down, "row", 1)
+    near_row = swap(to_near, "row", 0)
+    far_row = swap(to_far, "row", 1)
     d_keys, d_values, d_rel_bias = pl.pallas_call(
         final_body,
         out_shape=(shape(keys.shape), shape(keys.shape), shape(rel_bias.shape, jnp.float32)),
@@ -348,7 +357,7 @@
         out_specs=(VMEM, VMEM, VMEM),
         compiler_params=pltpu.CompilerParams(vmem_limit_bytes=LIMIT),
         name="final",
-    )(own, from_near, from_far, from_above, from_below, total)
+    )(own, from_near, from_far, near_row, far_row, total)
     return (attended, d_queries, d_keys, d_values, d_rel_bias)
 
 

time: 115 us -> 111 us (0.965)
  waiting for transfers between devices: 6.69 us -> 3.08 us
  starting transfers between devices: 39.6 us -> 37.4 us
  blocking collectives: 50.9 us -> 52.2 us
    ppermute x4 -> x0, starting transfers between devices: 29.5 us -> none  [neighbour(): lax.ppermute(value, axis, [(i, i + step) for i in range(size) if 0 <= i +...]
    ppermute x4 -> x8, starting transfers between devices: 10 us -> 37.4 us  [swap(): return lax.ppermute(value, axis, pairs + [(j, i) for i, j in pairs])]
    ppermute x4 -> x0, waiting for transfers between devices: 5.22 us -> none  [neighbour(): lax.ppermute(value, axis, [(i, i + step) for i in range(size) if 0 <= i +...]
    ppermute x4 -> x8, waiting for transfers between devices: 1.47 us -> 3.08 us  [swap(): return lax.ppermute(value, axis, pairs + [(j, i) for i, j in pairs])]
    select_n x0 -> x2, other arithmetic: none -> 1.41 us  [the longest x1 1.37 us: shards(): far_row = swap(jnp.where(even_row, upper, lower), 'row', 1)]
    all_to_all x3, blocking collectives: 50.9 us -> 52.2 us  [exchange(): return lax.all_to_all(value, axis, 0, 0)]
    another operation x1 -> x0, other arithmetic: 1.23 us -> none  [shards(): both = jnp.stack([keys, values])]
  transfers between devices with their start and end apart: 8 -> 8, of which waited for: 2 -> 3; matrix products, arithmetic and copies ran while one was open for 1% -> 1% of each run, Pallas kernels for 4% -> 5%
where the time goes in v4:
time: 111 us; the launch traced here: 110 us
  blocking collectives  52.2 us (47%)
  starting transfers between devices  37.4 us (34%)
  Pallas kernels  12.2 us (11%)
  waiting for transfers between devices  3.08 us (3%)
  other arithmetic  2.55 us (2%)
  local copies, waits for them, and re-layouts  1.81 us (2%)
    all_to_all x3, blocking collectives, exchange(): return lax.all_to_all(value, axis, 0, 0)  52.2 us
    ppermute x8, starting transfers between devices, swap(): return lax.ppermute(value, axis, pairs + [(j, i) for i, j in pairs])  37.4 us
    pallas_call x1, Pallas kernels, shards(): pl.pallas_call(attend_body, out_shape=(shape(queries.shape), shape(querie...  5.95 us
    pallas_call x1, Pallas kernels, shards(): pl.pallas_call(bias_body, grid=(heads,), out_shape=shape((heads, ROWS * S...  5.02 us
    ppermute x8, waiting for transfers between devices, swap(): return lax.ppermute(value, axis, pairs + [(j, i) for i, j in pairs])  3.08 us
  transfers between devices with their start and end apart: 8, of which 3 were waited for; matrix products, arithmetic and copies ran while one was open for 1% of the time, Pallas kernels for 5%

profile of v4, /device:TPU:4, one launch (start us, length us, event | category | flops | bytes accessed | tf_op | source)
XLA Modules:
  0.0 110.0 jit_solution(9707340503263371709)
XLA Ops:
  0.6 0.0 copy-start.1
  0.6 0.0 copy-start
  0.7 1.4 %broadcast_select_fusion.6 = (bf16[2,6,16,768]{3,2,1,0:T(8,128)(2,1)S(1)}, bf16[2,6,16,768]{3,2,1,0:T(8,128)(2,1)S(1)}) fusion(pred[]{:T(512)S(6)} %eq.9, bf16[1,8,16,768]{3,2,1,0:T(8,128)(2,1)} %bitcast.9, bf16[1,8,16,768]{3,2,1,0:T(8,128)(2,1)} %bitcast.7), kind=kLoop, calls=%fused_computation.11 | loop fusion | flops 737280 | bytes 983041 | tf_op jit(solution)/shard_map/jit(_where)/select_n | solution.py:286
  2.0 18.2 %collective-permute-start.1 = (bf16[2,6,16,768]{3,2,1,0:T(8,128)(2,1)S(1)}, bf16[2,6,16,768]{3,2,1,0:T(8,128)(2,1)S(1)}, u32[]{:S(2)}, u32[]{:S(2)}) collective-permute-start(bf16[2,6,16,768]{3,2,1,0:T(8,128)(2,1)S(1)} %get-tuple-element.61), channel_id=1, source_target_pairs={{32,64},{96,128},{160,192},{224,256},{288,320},{352,384},{416,448}... | collective-permute-start | bytes 884744 | tf_op jit(solution)/shard_map/ppermute | solution.py:259
  20.2 1.9 %collective-permute-start = (bf16[2,6,16,768]{3,2,1,0:T(8,128)(2,1)S(1)}, bf16[2,6,16,768]{3,2,1,0:T(8,128)(2,1)S(1)}, u32[]{:S(2)}, u32[]{:S(2)}) collective-permute-start(bf16[2,6,16,768]{3,2,1,0:T(8,128)(2,1)S(1)} %get-tuple-element.62), channel_id=1, source_target_pairs={{0,32},{64,96},{128,160},{192,224},{256,288},{320,352},{384,416},{... | collective-permute-start | bytes 884744 | tf_op jit(solution)/shard_map/ppermute | solution.py:259
  22.2 1.0 copy.12
  23.2 0.0 copy-start.4
  23.2 0.7 copy-done.4
  23.9 0.0 copy-start.2
  23.9 0.0 copy-start.3
  23.9 5.0 %bias_mask.1.bias_ref = f32[12,640,128]{2,1,0:T(8,128)S(1)} custom-call(s32[2,16,32]{2,1,0:T(8,128)S(1)} %copy-done.4, f32[12,16,16]{2,1,0:T(8,128)S(1)} %pad.4.table_ref), custom_call_target="tpu_custom_call" | custom-call | flops 20000000 | bytes 4000000 | tf_op jit(solution)/shard_map/bias_mask/pallas_call | solution.py:289
  29.0 0.7 collective-permute-done.1.far_row_ref
  29.7 0.9 collective-permute-done.near_row_ref
  30.6 0.0 copy-done.1
  30.6 0.0 copy-done
  30.6 0.1 pad_maximum_fusion
  30.8 0.1 broadcast_select_fusion.2
  30.8 0.7 collective-permute-start.3
  31.5 4.8 %collective-permute-start.2 = (bf16[2,20,8,768]{3,2,1,0:T(8,128)(2,1)S(1)}, bf16[2,20,8,768]{3,2,1,0:T(8,128)(2,1)S(1)}, u32[]{:S(2)}, u32[]{:S(2)}) collective-permute-start(bf16[2,20,8,768]{3,2,1,0:T(8,128)(2,1)S(1)} %get-tuple-element.58), channel_id=1, source_target_pairs={{0,1},{2,3},{4,5},{6,7},{8,9},{10,11},{12,13},{14,15},{16,17},{18,... | collective-permute-start | bytes 1474568 | tf_op jit(solution)/shard_map/ppermute | solution.py:259
  36.4 0.0 collective-permute-done.3.far_ref
  36.4 1.5 %collective-permute-done.2.near_ref = bf16[2,20,8,768]{3,2,1,0:T(8,128)(2,1)S(1)} collective-permute-done((bf16[2,20,8,768]{3,2,1,0:T(8,128)(2,1)S(1)}, bf16[2,20,8,768]{3,2,1,0:T(8,128)(2,1)S(1)}, u32[]{:S(2)}, u32[]{:S(2)}) %collective-permute-start.2) | collective-permute-done | bytes 491552 | tf_op jit(solution)/shard_map/ppermute | solution.py:259
  37.8 0.0 copy-done.2
  37.8 0.0 copy-done.3
  37.8 5.9 %attend.1 = (bf16[8,16,768]{2,1,0:T(8,128)(2,1)}, bf16[8,16,768]{2,1,0:T(8,128)(2,1)}, f32[2,8,16,768]{3,2,1,0:T(8,128)S(1)}, f32[2,6,16,768]{3,2,1,0:T(8,128)S(...) custom-call(s32[2,16,32]{2,1,0:T(8,128)S(1)} %copy-done.4, ...), custom_call_target="tpu_custom_call" | custom-call | flops 1500000000 | bytes 9000000 | tf_op jit(solution)/shard_map/attend/pallas_call | solution.py:309
  43.8 21.6 %all_to_all.15 = f32[32,1,128]{2,1,0:T(1,128)S(1)} all-to-all(f32[32,1,128]{2,1,0:T(1,128)S(1)} %bitcast.12), channel_id=1, replica_groups=mesh['row'=32,'col'=32] {'col'}, dimensions={0} | all-to-all | bytes 32768 | tf_op jit(solution)/shard_map/all_to_all | solution.py:263
  65.4 0.9 broadcast_select_fusion
  66.2 0.7 collective-permute-start.5
  66.9 3.8 %collective-permute-start.4 = (bf16[2,20,8,768]{3,2,1,0:T(8,128)(2,1)S(1)}, bf16[2,20,8,768]{3,2,1,0:T(8,128)(2,1)S(1)}, u32[]{:S(2)}, u32[]{:S(2)}) collective-permute-start(bf16[2,20,8,768]{3,2,1,0:T(8,128)(2,1)S(1)} %get-tuple-element.56), channel_id=1, source_target_pairs={{0,1},{2,3},{4,5},{6,7},{8,9},{10,11},{12,13},{14,15},{16,17},{18,... | collective-permute-start | bytes 1474568 | tf_op jit(solution)/shard_map/ppermute | solution.py:259
  70.8 0.1 reduce_sum.18
  70.8 18.1 %all_to_all.16 = f32[32,1,128]{2,1,0:T(1,128)S(1)} all-to-all(f32[32,1,128]{2,1,0:T(1,128)S(1)} %broadcast_in_dim.6), channel_id=1, replica_groups=mesh['row'=32,'col'=32] {'row'}, dimensions={0} | all-to-all | bytes 32768 | tf_op jit(solution)/shard_map/all_to_all | solution.py:263
  88.9 0.0 collective-permute-done.5.far_ref
  88.9 0.0 collective-permute-done.4.near_ref
  88.9 0.2 border.1
  89.2 2.4 %collective-permute-start.6 = (bf16[2,6,16,768]{3,2,1,0:T(8,128)(2,1)S(1)}, bf16[2,6,16,768]{3,2,1,0:T(8,128)(2,1)S(1)}, u32[]{:S(2)}, u32[]{:S(2)}) collective-permute-start(bf16[2,6,16,768]{3,2,1,0:T(8,128)(2,1)S(1)} %get-tuple-element.49), channel_id=1, source_target_pairs={{0,32},{64,96},{128,160},{192,224},{256,288},{320,352},{384,416},{... | collective-permute-start | bytes 884744 | tf_op jit(solution)/shard_map/ppermute | solution.py:259
  91.6 4.9 %collective-permute-start.7 = (bf16[2,6,16,768]{3,2,1,0:T(8,128)(2,1)S(1)}, bf16[2,6,16,768]{3,2,1,0:T(8,128)(2,1)S(1)}, u32[]{:S(2)}, u32[]{:S(2)}) collective-permute-start(bf16[2,6,16,768]{3,2,1,0:T(8,128)(2,1)S(1)} %get-tuple-element.50), channel_id=1, source_target_pairs={{32,64},{96,128},{160,192},{224,256},{288,320},{352,384},{416,448}... | collective-permute-start | bytes 884744 | tf_op jit(solution)/shard_map/ppermute | solution.py:259
  96.5 0.1 reduce_sum.19
  96.6 12.5 %all_to_all.17 = f32[32,1,128]{2,1,0:T(1,128)S(1)} all-to-all(f32[32,1,128]{2,1,0:T(1,128)S(1)} %broadcast_in_dim.7), channel_id=1, replica_groups=mesh['row'=32,'col'=32] {'col'}, dimensions={0} | all-to-all | bytes 32768 | tf_op jit(solution)/shard_map/all_to_all | solution.py:263
  109.1 0.0 collective-permute-done.6.near_row_ref
  109.1 0.0 collective-permute-done.7.far_row_ref
  109.1 1.0 final.1
  (4 shorter events, 0.1 us)
Async XLA Ops:
  0.6 30.0 %copy-start.1 = (bf16[8,16,768]{2,1,0:T(8,128)(2,1)S(1)}, bf16[8,16,768]{2,1,0:T(8,128)(2,1)}, u32[]{:S(2)}) copy-start(bf16[8,16,768]{2,1,0:T(8,128)(2,1)} %v_ref.1) | copy-start | bytes 589828
  0.6 30.0 %copy-start = (bf16[8,16,768]{2,1,0:T(8,128)(2,1)S(1)}, bf16[8,16,768]{2,1,0:T(8,128)(2,1)}, u32[]{:S(2)}) copy-start(bf16[8,16,768]{2,1,0:T(8,128)(2,1)} %k_ref.1) | copy-start | bytes 589828
  2.0 27.7 %collective-permute-start.1 = (bf16[2,6,16,768]{3,2,1,0:T(8,128)(2,1)S(1)}, bf16[2,6,16,768]{3,2,1,0:T(8,128)(2,1)S(1)}, u32[]{:S(2)}, u32[]{:S(2)}) collective-permute-start(bf16[2,6,16,768]{3,2,1,0:T(8,128)(2,1)S(1)} %get-tuple-element.61), channel_id=1, source_target_pairs={{32,64},{96,128},{160,192},{224,256},{288,320},{352,384},{416,448}... | collective-permute-start | bytes 884744 | tf_op jit(solution)/shard_map/ppermute | solution.py:259
  20.2 10.4 %collective-permute-start = (bf16[2,6,16,768]{3,2,1,0:T(8,128)(2,1)S(1)}, bf16[2,6,16,768]{3,2,1,0:T(8,128)(2,1)S(1)}, u32[]{:S(2)}, u32[]{:S(2)}) collective-permute-start(bf16[2,6,16,768]{3,2,1,0:T(8,128)(2,1)S(1)} %get-tuple-element.62), channel_id=1, source_target_pairs={{0,32},{64,96},{128,160},{192,224},{256,288},{320,352},{384,416},{... | collective-permute-start | bytes 884744 | tf_op jit(solution)/shard_map/ppermute | solution.py:259
  23.2 0.7 copy-start.4
  23.9 13.9 %copy-start.2 = (bf16[8,16,768]{2,1,0:T(8,128)(2,1)S(1)}, bf16[8,16,768]{2,1,0:T(8,128)(2,1)}, u32[]{:S(2)}) copy-start(bf16[8,16,768]{2,1,0:T(8,128)(2,1)} %q_ref.1) | copy-start | bytes 589828
  23.9 13.9 %copy-start.3 = (bf16[8,16,768]{2,1,0:T(8,128)(2,1)S(1)}, bf16[8,16,768]{2,1,0:T(8,128)(2,1)}, u32[]{:S(2)}) copy-start(bf16[8,16,768]{2,1,0:T(8,128)(2,1)} %g_ref.1) | copy-start | bytes 589828
  30.8 5.5 %collective-permute-start.3 = (bf16[2,20,8,768]{3,2,1,0:T(8,128)(2,1)S(1)}, bf16[2,20,8,768]{3,2,1,0:T(8,128)(2,1)S(1)}, u32[]{:S(2)}, u32[]{:S(2)}) collective-permute-start(bf16[2,20,8,768]{3,2,1,0:T(8,128)(2,1)S(1)} %get-tuple-element.57), channel_id=1, source_target_pairs={{1,2},{3,4},{5,6},{7,8},{9,10},{11,12},{13,14},{15,16},{17,18},{19... | collective-permute-start | bytes 1474568 | tf_op jit(solution)/shard_map/ppermute | solution.py:259
  31.5 6.3 %collective-permute-start.2 = (bf16[2,20,8,768]{3,2,1,0:T(8,128)(2,1)S(1)}, bf16[2,20,8,768]{3,2,1,0:T(8,128)(2,1)S(1)}, u32[]{:S(2)}, u32[]{:S(2)}) collective-permute-start(bf16[2,20,8,768]{3,2,1,0:T(8,128)(2,1)S(1)} %get-tuple-element.58), channel_id=1, source_target_pairs={{0,1},{2,3},{4,5},{6,7},{8,9},{10,11},{12,13},{14,15},{16,17},{18,... | collective-permute-start | bytes 1474568 | tf_op jit(solution)/shard_map/ppermute | solution.py:259
  66.2 22.7 %collective-permute-start.5 = (bf16[2,20,8,768]{3,2,1,0:T(8,128)(2,1)}, bf16[2,20,8,768]{3,2,1,0:T(8,128)(2,1)S(1)}, u32[]{:S(2)}, u32[]{:S(2)}) collective-permute-start(bf16[2,20,8,768]{3,2,1,0:T(8,128)(2,1)} %get-tuple-element.55), channel_id=1, source_target_pairs={{1,2},{3,4},{5,6},{7,8},{9,10},{11,12},{13,14},{15,16},{17,18},{19... | collective-permute-start | bytes 1474568 | tf_op jit(solution)/shard_map/ppermute | solution.py:259
  66.9 22.0 %collective-permute-start.4 = (bf16[2,20,8,768]{3,2,1,0:T(8,128)(2,1)S(1)}, bf16[2,20,8,768]{3,2,1,0:T(8,128)(2,1)S(1)}, u32[]{:S(2)}, u32[]{:S(2)}) collective-permute-start(bf16[2,20,8,768]{3,2,1,0:T(8,128)(2,1)S(1)} %get-tuple-element.56), channel_id=1, source_target_pairs={{0,1},{2,3},{4,5},{6,7},{8,9},{10,11},{12,13},{14,15},{16,17},{18,... | collective-permute-start | bytes 1474568 | tf_op jit(solution)/shard_map/ppermute | solution.py:259
  89.2 19.9 %collective-permute-start.6 = (bf16[2,6,16,768]{3,2,1,0:T(8,128)(2,1)S(1)}, bf16[2,6,16,768]{3,2,1,0:T(8,128)(2,1)S(1)}, u32[]{:S(2)}, u32[]{:S(2)}) collective-permute-start(bf16[2,6,16,768]{3,2,1,0:T(8,128)(2,1)S(1)} %get-tuple-element.49), channel_id=1, source_target_pairs={{0,32},{64,96},{128,160},{192,224},{256,288},{320,352},{384,416},{... | collective-permute-start | bytes 884744 | tf_op jit(solution)/shard_map/ppermute | solution.py:259
  91.6 17.4 %collective-permute-start.7 = (bf16[2,6,16,768]{3,2,1,0:T(8,128)(2,1)S(1)}, bf16[2,6,16,768]{3,2,1,0:T(8,128)(2,1)S(1)}, u32[]{:S(2)}, u32[]{:S(2)}) collective-permute-start(bf16[2,6,16,768]{3,2,1,0:T(8,128)(2,1)S(1)} %get-tuple-element.50), channel_id=1, source_target_pairs={{32,64},{96,128},{160,192},{224,256},{288,320},{352,384},{416,448}... | collective-permute-start | bytes 884744 | tf_op jit(solution)/shard_map/ppermute | solution.py:259
